TPU v7x, 512 devices: a whole 4x4x16 slice. The times are simulated.
512 devices in a mesh: head: 8 (over y, core), frame: 64 (over x, z).
Axes of the slice: x: 4, y: 4, z: 16, core: 2. Of those that a mesh axis runs over, the one named last changes fastest.
Arguments:
- queries: bfloat16 [65536, 16, 128], P(('frame', 'head')), may hold values from -30 to 30
- keys: bfloat16 [65536, 16, 128], P(('frame', 'head')), may hold values from -4 to 4
- values: bfloat16 [65536, 16, 128], P(('frame', 'head')), may hold values from -24 to 24
- block_mask: int32 [64, 16, 16], replicated, may hold values from 0 to 1, as said below
- strides: int32 [64], replicated, may hold values from 1 to 16, as said below
- offsets: int32 [64], replicated, may hold values from 0 to 15
Outputs:
- attended: bfloat16 [65536, 16, 128], P(('frame', 'head'))
Inputs may be any that keep to these rules, and one draw needn't show every extreme that they name: Every diagonal entry block_mask[i, b, b] is 1. strides[0] is 1, strides[1] is 4, 8 or 16, and every later entry is 8 or 16.
All inputs are finite; a program needn't handle non-finite values.
Results may differ from a plain program's by a relative error of at most 0.0043.
Values may be sent and summed in bfloat16 or wider, within the bound.
No kernel may reach another device: no remote copies, remote signals or barrier semaphores. Data moves between devices by JAX's collectives and lax.ppermute only.
A program may use at most 64 MiB of HBM per device.

v0:
```python
import jax
import jax.numpy as jnp
from jax import lax
from jax.sharding import PartitionSpec as P

masked_score = -1e30


def passed_along(block, axis, distance):
    devices = range(lax.axis_size(axis))
    route = [(i - distance, i) for i in devices if i - distance in devices]
    return lax.ppermute(block, axis, route)


def group_terms(query_blocks, key_rows, value_rows, keep_mask, score_scale):
    scores = (
        jnp.einsum("qahd,gnhd->hqagn", query_blocks, key_rows, preferred_element_type=jnp.float32)
        * score_scale
    )
    allowed = keep_mask[None, :, None, :, :]
    scores = jnp.where(allowed, scores, masked_score)
    group_tops = jnp.max(scores, axis=4)
    weights = jnp.where(allowed, jnp.exp(scores - group_tops[..., None]), 0.0)
    group_totals = jnp.sum(weights, axis=4)
    group_sums = jnp.einsum(
        "hqagn,gnhd->hqagd",
        weights.astype(jnp.bfloat16),
        value_rows,
        preferred_element_type=jnp.float32,
    )
    return (group_tops, group_totals, group_sums)


def absorb(carry_state, group_tops, group_totals, group_sums):
    running_top, running_total, running_sum = carry_state
    new_top = jnp.maximum(running_top, jnp.max(group_tops, axis=3))
    shrink = jnp.exp(running_top - new_top)
    factors = jnp.exp(group_tops - new_top[..., None])
    running_total = running_total * shrink + jnp.sum(factors * group_totals, axis=3)
    running_sum = running_sum * shrink[..., None] + jnp.sum(factors[..., None] * group_sums, axis=3)
    return (new_top, running_total, running_sum)


def pick_blocks(key_blocks, value_blocks, offsets, source_frame, spacing, block_count):
    first_block = (spacing - offsets[source_frame] % spacing) % spacing
    chosen = first_block + spacing * jnp.arange(block_count, dtype=jnp.int32)
    return jnp.stack([jnp.take(key_blocks, chosen, axis=0), jnp.take(value_blocks, chosen, axis=0)])


def local(queries, keys, values, block_mask, strides, offsets):
    local_queries, local_keys, local_values = (
        lax.all_to_all(queries, "head", split_axis=1, concat_axis=0, tiled=True),
        lax.all_to_all(keys, "head", split_axis=1, concat_axis=0, tiled=True),
        lax.all_to_all(values, "head", split_axis=1, concat_axis=0, tiled=True),
    )
    frame_rows, heads_here, head_dim = local_queries.shape
    frame_blocks = block_mask.shape[1]
    block_rows = frame_rows // frame_blocks
    score_scale = head_dim ** (-0.5)
    frame_index = lax.axis_index("frame")
    frame_total = lax.axis_size("frame")
    query_blocks = local_queries.reshape(frame_blocks, block_rows, heads_here, head_dim)
    key_blocks = local_keys.reshape(frame_blocks, block_rows, heads_here, head_dim)
    value_blocks = local_values.reshape(frame_blocks, block_rows, heads_here, head_dim)
    own_mask = lax.dynamic_index_in_dim(block_mask, frame_index, 0, keepdims=False) == 1
    carry_state = (
        jnp.full((heads_here, frame_blocks, block_rows), masked_score, jnp.float32),
        jnp.zeros((heads_here, frame_blocks, block_rows), jnp.float32),
        jnp.zeros((heads_here, frame_blocks, block_rows, head_dim), jnp.float32),
    )
    half_blocks = frame_blocks // 2
    whole_keys = local_keys.reshape(1, frame_rows, heads_here, head_dim)
    whole_values = local_values.reshape(1, frame_rows, heads_here, head_dim)
    results = []
    for first_block in (0, half_blocks):
        keep_mask = jnp.repeat(
            own_mask[first_block : first_block + half_blocks], block_rows, axis=1
        )[:, None, :]
        results.append(
            group_terms(
                query_blocks[first_block : first_block + half_blocks],
                whole_keys,
                whole_values,
                keep_mask,
                score_scale,
            )
        )
    carry_state = absorb(
        carry_state,
        jnp.concatenate([entry[0] for entry in results], axis=1),
        jnp.concatenate([entry[1] for entry in results], axis=1),
        jnp.concatenate([entry[2] for entry in results], axis=1),
    )
    for distance in (1, 2, 3):
        spacing = frame_blocks // 4 if distance == 1 else frame_blocks // 2
        block_count = frame_blocks // spacing
        packed = pick_blocks(key_blocks, value_blocks, offsets, frame_index, spacing, block_count)
        for direction in (1, -1):
            arrived = passed_along(packed, "frame", direction * distance)
            source_frame = frame_index - direction * distance
            valid = (source_frame >= 0) & (source_frame < frame_total)
            clipped = jnp.clip(source_frame, 0, frame_total - 1)
            chosen = (spacing - offsets[clipped] % spacing) % spacing + spacing * jnp.arange(
                block_count, dtype=jnp.int32
            )
            attend_phase_ok = (chosen + offsets[clipped]) % strides[distance] == 0
            attend_kept = valid & own_mask[:, chosen] & attend_phase_ok[None, :]
            attend_keep_mask = jnp.repeat(attend_kept, block_rows, axis=1)[:, None, :]
            near_keys = arrived[0].reshape(1, block_count * block_rows, heads_here, head_dim)
            near_values = arrived[1].reshape(1, block_count * block_rows, heads_here, head_dim)
            carry_state = absorb(
                carry_state,
                *group_terms(query_blocks, near_keys, near_values, attend_keep_mask, score_scale)
            )
    anchor_block = (frame_blocks - offsets[frame_index] % frame_blocks) % frame_blocks
    anchor_pair = jnp.stack([key_blocks[anchor_block], value_blocks[anchor_block]])[None]
    gathered = lax.all_gather(anchor_pair, "frame", axis=0, tiled=True)
    piece_frames = gathered.shape[0]
    group_width = 4
    grouped = gathered.reshape(
        piece_frames // group_width, group_width, 2, block_rows, heads_here, head_dim
    )

    def one_group(state_inner, entry):
        group_blocks, group_number = entry
        sources = 0 + group_number * group_width + jnp.arange(group_width, dtype=jnp.int32)
        distances = jnp.abs(frame_index - sources)
        spots = (frame_blocks - offsets[sources] % frame_blocks) % frame_blocks
        phase_ok = (spots + offsets[sources]) % strides[distances] == 0
        kept = (distances >= 4)[None, :] & own_mask[:, spots] & phase_ok[None, :]
        keep_mask = jnp.repeat(kept, block_rows, axis=1).reshape(
            frame_blocks, group_width, block_rows
        )
        terms = group_terms(
            query_blocks, group_blocks[:, 0], group_blocks[:, 1], keep_mask, score_scale
        )
        return (absorb(state_inner, *terms), None)

    numbers = jnp.arange(piece_frames // group_width, dtype=jnp.int32)
    state_out, unused = lax.scan(one_group, carry_state, (grouped, numbers))
    carry_state = state_out
    running_top, running_total, running_sum = carry_state
    output = (running_sum / running_total[..., None]).astype(jnp.bfloat16)
    output = jnp.transpose(output, (1, 2, 0, 3)).reshape(frame_rows, heads_here, head_dim)
    return lax.all_to_all(output, "head", split_axis=0, concat_axis=1, tiled=True)


def solution(mesh):
    placed = (
        P(("frame", "head"), None, None),
        P(("frame", "head"), None, None),
        P(("frame", "head"), None, None),
        P(),
        P(),
        P(),
    )
    return jax.shard_map(
        local,
        mesh=mesh,
        in_specs=placed,
        out_specs=P(("frame", "head"), None, None),
        check_vma=False,
    )
```

profile of v0, /device:TPU:1, one launch (start us, length us, event | category | flops | bytes accessed | tf_op | source)
XLA Modules:
  0.0 511.0 jit_solution(10326645621186077479)
XLA Ops:
  8.6 10.2 %all-to-all-start.1 = ((bf16[128,16,128]{2,0,1:T(8,128)(2,1)}), bf16[128,16,128]{2,0,1:T(8,128)(2,1)S(1)}, u32[]{:S(2)}, u32[]{:S(2)}) async-start(bf16[128,16,128]{2,0,1:T(8,128)(2,1)} %copy.119), calls=%async_computation.1 | async-start | bytes 1048576 | tf_op jit(solution)/shard_map/all_to_all | solution.py:53
  49.3 4.8 all-to-all-start.2
  61.0 2.5 all-to-all-done.2
  63.5 4.4 all-to-all-start
  71.7 4.0 collective-permute-start
  79.0 7.0 %collective-permute-start.4 = (bf16[2,2,64,2,128]{4,2,3,1,0:T(8,128)(2,1)S(1)}, bf16[2,2,64,2,128]{4,2,3,1,0:T(8,128)(2,1)S(1)}, u32[]{:S(2)}, u32[]{:S(2)}) collective-permute-start(bf16[2,2,64,2,128]{4,2,3,1,0:T(8,128)(2,1)S(1)} %pad_maximum_fusion.1), channel_id=1, source_target_pairs={{0,3},{1,4},{2,5},{3,6},{4,7},{5,8},{6,9},{7,10},{8,11},{9,12},{10... | collective-permute-start | bytes 393224 | tf_op jit(solution)/shard_map/ppermute | solution.py:12
  90.2 2.7 fusion.21
  97.3 7.7 %collective-permute-done.3 = bf16[2,2,64,2,128]{4,2,3,1,0:T(8,128)(2,1)S(1)} collective-permute-done((bf16[2,2,64,2,128]{4,2,3,1,0:T(8,128)(2,1)S(1)}, bf16[2,2,64,2,128]{4,2,3,1,0:T(8,128)(2,1)S(1)}, u32[]{:S(2)}, u32[]{:S(2)}) %collective-permute-start.3) | collective-permute-done | bytes 131104 | tf_op jit(solution)/shard_map/ppermute | solution.py:12
  120.8 3.0 fusion.58
  123.7 103.3 %all-gather.3.cloned.1.call-done = bf16[128,64,2,128]{3,1,0,2:T(8,128)(2,1)} async-done(((bf16[2,64,2,128]{3,1,0,2:T(8,128)(2,1)}), bf16[128,64,2,128]{3,1,0,2:T(8,128)(2,1)}) %all-gather.3.cloned.1.call-update) | async-done | bytes 4194320 | tf_op jit(solution)/shard_map/all_gather | solution.py:117
  227.0 250.4 %while.16 = (s32[]{:T(128)}, f32[2,16,64]{2,1,0:T(8,128)S(1)}, f32[2,16,64]{2,1,0:T(8,128)S(1)}, f32[2,16,64,128]{3,2,1,0:T(8,128)}, s32[]{:T(128)}, /*index=5*/...) while((s32[]{:T(128)}, f32[2,16,64]{2,1,0:T(8,128)S(1)}, ...), condition=%wide.region_22.25_spmd, body=%wide.region_16.24_spmd.sunk | while | flops 276053440 | bytes 31036728 | solution.py:140
  234.9 2.7 copy.175
  248.1 2.4 fusion.229
  250.5 2.7 copy.175
  263.7 2.4 fusion.229
  266.2 2.7 copy.175
  279.4 2.4 fusion.229
  281.8 2.7 copy.175
  295.0 2.4 fusion.229
  297.5 2.7 copy.175
  313.1 2.7 copy.175
  328.8 2.7 copy.175
  344.4 2.7 copy.175
  360.1 2.7 copy.175
  375.7 2.7 copy.175
  391.4 2.7 copy.175
  407.0 2.7 copy.175
  422.7 2.7 copy.175
  438.3 2.7 copy.175
  453.9 2.7 copy.175
  469.6 2.7 copy.175
  479.5 23.4 %all_to_all.63 = bf16[1024,2,128]{2,1,0:T(2,128)(2,1)S(1)} all-to-all(bf16[1024,2,128]{2,1,0:T(2,128)(2,1)S(1)} %bitcast.475), channel_id=1, replica_groups=mesh['head'=8,'frame'=64] {'head'}, dimensions={0} | all-to-all | bytes 1048576 | tf_op jit(solution)/shard_map/all_to_all | solution.py:145
  (580 shorter events, 242.5 us)
Async XLA Ops:
  6.5 33.9 %copy-start = (s32[64,16,16]{0,2,1:T(8,128)S(1)}, s32[64,16,16]{0,2,1:T(8,128)}, u32[]{:S(2)}) copy-start(s32[64,16,16]{0,2,1:T(8,128)} %param.15) | copy-start | bytes 196612
  6.5 47.7 %copy-start.5 = (bf16[128,16,128]{2,1,0:T(8,128)(2,1)S(1)}, bf16[128,16,128]{2,1,0:T(8,128)(2,1)}, u32[]{:S(2)}) copy-start(bf16[128,16,128]{2,1,0:T(8,128)(2,1)} %param.12) | copy-start | bytes 1572868
  8.6 40.7 %all-to-all-start.1 = ((bf16[128,16,128]{2,0,1:T(8,128)(2,1)}), bf16[128,16,128]{2,0,1:T(8,128)(2,1)S(1)}, u32[]{:S(2)}, u32[]{:S(2)}) async-start(bf16[128,16,128]{2,0,1:T(8,128)(2,1)} %copy.119), calls=%async_computation.1 | async-start | bytes 1048576 | tf_op jit(solution)/shard_map/all_to_all | solution.py:53
  49.3 14.2 %all-to-all-start.2 = ((bf16[128,16,128]{2,0,1:T(8,128)(2,1)}), bf16[128,16,128]{2,0,1:T(8,128)(2,1)S(1)}, u32[]{:S(2)}, u32[]{:S(2)}) async-start(bf16[128,16,128]{2,0,1:T(8,128)(2,1)} %copy.125), calls=%async_computation.2 | async-start | bytes 1048576 | tf_op jit(solution)/shard_map/all_to_all | solution.py:54
  63.5 22.5 %all-to-all-start = ((bf16[128,16,128]{2,0,1:T(8,128)(2,1)}), bf16[128,16,128]{2,0,1:T(8,128)(2,1)S(1)}, u32[]{:S(2)}, u32[]{:S(2)}) async-start(bf16[128,16,128]{2,0,1:T(8,128)(2,1)} %copy.117), calls=%async_computation | async-start | bytes 1048576 | tf_op jit(solution)/shard_map/all_to_all | solution.py:52
  67.8 159.2 %all-gather.3.cloned.1.call-start = ((), (), s32[]{:S(2)}) async-start(), calls=%async_computation.4 | async-start | bytes 4259840 | tf_op jit(solution)/shard_map/all_gather | solution.py:117
  70.4 40.1 %collective-permute-start.1 = (bf16[2,4,64,2,128]{4,2,3,1,0:T(8,128)(2,1)S(1)}, bf16[2,4,64,2,128]{4,2,3,1,0:T(8,128)(2,1)S(1)}, u32[]{:S(2)}, u32[]{:S(2)}) collective-permute-start(bf16[2,4,64,2,128]{4,2,3,1,0:T(8,128)(2,1)S(1)} %pad_maximum_fusion), channel_id=1, source_target_pairs={{1,0},{2,1},{3,2},{4,3},{5,4},{6,5},{7,6},{8,7},{9,8},{10,9},{11,1... | collective-permute-start | bytes 786440 | tf_op jit(solution)/shard_map/ppermute | solution.py:12
  71.7 38.8 %collective-permute-start = (bf16[2,4,64,2,128]{4,2,3,1,0:T(8,128)(2,1)S(1)}, bf16[2,4,64,2,128]{4,2,3,1,0:T(8,128)(2,1)S(1)}, u32[]{:S(2)}, u32[]{:S(2)}) collective-permute-start(bf16[2,4,64,2,128]{4,2,3,1,0:T(8,128)(2,1)S(1)} %pad_maximum_fusion), channel_id=1, source_target_pairs={{0,1},{1,2},{2,3},{3,4},{4,5},{5,6},{6,7},{7,8},{8,9},{9,10},{10,1... | collective-permute-start | bytes 786440 | tf_op jit(solution)/shard_map/ppermute | solution.py:12
  75.8 18.2 %collective-permute-start.2 = (bf16[2,2,64,2,128]{4,2,3,1,0:T(8,128)(2,1)S(1)}, bf16[2,2,64,2,128]{4,2,3,1,0:T(8,128)(2,1)}, u32[]{:S(2)}, u32[]{:S(2)}) collective-permute-start(bf16[2,2,64,2,128]{4,2,3,1,0:T(8,128)(2,1)S(1)} %pad_maximum_fusion.1), channel_id=1, source_target_pairs={{0,2},{1,3},{2,4},{3,5},{4,6},{5,7},{6,8},{7,9},{8,10},{9,11},{10,... | collective-permute-start | bytes 393224 | tf_op jit(solution)/shard_map/ppermute | solution.py:12
  77.7 18.7 %collective-permute-start.5 = (bf16[2,2,64,2,128]{4,2,3,1,0:T(8,128)(2,1)S(1)}, bf16[2,2,64,2,128]{4,2,3,1,0:T(8,128)(2,1)}, u32[]{:S(2)}, u32[]{:S(2)}) collective-permute-start(bf16[2,2,64,2,128]{4,2,3,1,0:T(8,128)(2,1)S(1)} %pad_maximum_fusion.1), channel_id=1, source_target_pairs={{3,0},{4,1},{5,2},{6,3},{7,4},{8,5},{9,6},{10,7},{11,8},{12,9},{13... | collective-permute-start | bytes 393224 | tf_op jit(solution)/shard_map/ppermute | solution.py:12
  79.0 18.3 %collective-permute-start.4 = (bf16[2,2,64,2,128]{4,2,3,1,0:T(8,128)(2,1)S(1)}, bf16[2,2,64,2,128]{4,2,3,1,0:T(8,128)(2,1)S(1)}, u32[]{:S(2)}, u32[]{:S(2)}) collective-permute-start(bf16[2,2,64,2,128]{4,2,3,1,0:T(8,128)(2,1)S(1)} %pad_maximum_fusion.1), channel_id=1, source_target_pairs={{0,3},{1,4},{2,5},{3,6},{4,7},{5,8},{6,9},{7,10},{8,11},{9,12},{10... | collective-permute-start | bytes 393224 | tf_op jit(solution)/shard_map/ppermute | solution.py:12
  92.9 12.5 %copy-start.11 = (pred[16,128]{1,0:T(8,128)(4,1)S(1)}, pred[16,128]{1,0:T(8,128)(4,1)}, u32[]{:S(2)}) copy-start(pred[16,128]{1,0:T(8,128)(4,1)} %broadcast_in_dim.280) | copy-start | bytes 6148
  94.0 12.1 %copy-start.9 = (pred[16,128]{1,0:T(8,128)(4,1)S(1)}, pred[16,128]{1,0:T(8,128)(4,1)}, u32[]{:S(2)}) copy-start(pred[16,128]{1,0:T(8,128)(4,1)} %broadcast_in_dim.277) | copy-start | bytes 6148
  94.0 11.1 %collective-permute-start.3 = (bf16[2,2,64,2,128]{4,2,3,1,0:T(8,128)(2,1)S(1)}, bf16[2,2,64,2,128]{4,2,3,1,0:T(8,128)(2,1)S(1)}, u32[]{:S(2)}, u32[]{:S(2)}) collective-permute-start(bf16[2,2,64,2,128]{4,2,3,1,0:T(8,128)(2,1)S(1)} %pad_maximum_fusion.1), channel_id=1, source_target_pairs={{2,0},{3,1},{4,2},{5,3},{6,4},{7,5},{8,6},{9,7},{10,8},{11,9},{12,... | collective-permute-start | bytes 393224 | tf_op jit(solution)/shard_map/ppermute | solution.py:12
  96.4 10.3 %copy-start.10 = (pred[16,128]{1,0:T(8,128)(4,1)S(1)}, pred[16,128]{1,0:T(8,128)(4,1)}, u32[]{:S(2)}) copy-start(pred[16,128]{1,0:T(8,128)(4,1)} %broadcast_in_dim.274) | copy-start | bytes 6148
  106.1 3.3 copy-start.8
  120.7 106.3 %copy-start.1 = (s32[64]{0:T(128)S(1)}, s32[64]{0:T(128)}, u32[]{:S(2)}) copy-start(s32[64]{0:T(128)} %param.17) | copy-start | bytes 772
  120.7 106.3 %copy-start.2 = (s32[64]{0:T(128)S(1)}, s32[64]{0:T(128)}, u32[]{:S(2)}) copy-start(s32[64]{0:T(128)} %param.16) | copy-start | bytes 772
  239.8 1.3 copy-start.3
  255.5 1.3 copy-start.3
  271.1 1.3 copy-start.3
  286.8 1.3 copy-start.3
  302.4 1.3 copy-start.3
  318.1 1.3 copy-start.3
  333.7 1.3 copy-start.3
  349.4 1.3 copy-start.3
  365.0 1.3 copy-start.3
  380.6 1.3 copy-start.3
  396.3 1.3 copy-start.3
  411.9 1.3 copy-start.3
  443.2 1.3 copy-start.3
  458.9 1.3 copy-start.3
  (20 other events, 21.1 us)
Sparse Core Ops, SparseCore 0:
  86.9 140.0 all-gather.2
where the time goes:
time: 513 us; the launch traced here: 511 us
  local copies, waits for them, and re-layouts  137 us (27%)
  waiting for transfers between devices  114 us (22%)
  other arithmetic  89 us (17%)
  matrix products  68.6 us (13%)
  starting transfers between devices  36.4 us (7%)
  between operations  31 us (6%)
  blocking collectives  23.4 us (5%)
  loops' own time  12.5 us (2%)
    all_gather x1, waiting for transfers between devices, local(): gathered = lax.all_gather(anchor_pair, 'frame', axis=0, tiled=True)  103 us
    reduce_sum x23, other arithmetic, group_terms(): group_totals = jnp.sum(weights, axis=4)  45.4 us
    convert_element_type x16, local copies, waits for them, and re-layouts, group_terms(): weights.astype(jnp.bfloat16)  42.6 us
    while x16, matrix products  36.3 us
    all_to_all x1, blocking collectives, local(): lax.all_to_all(output, 'head', split_axis=0, concat_axis=1, tiled=True)  23.4 us
    reduce_sum x16, other arithmetic, absorb(): jnp.sum(factors[..., None] * group_sums, axis=3)  21 us
    dot_general x18, matrix products, group_terms(): jnp.einsum('qahd,gnhd->hqagn', query_blocks, key_rows, preferred_element_...  19 us
    ppermute x6, starting transfers between devices, passed_along(): return lax.ppermute(block, axis, route)  16.9 us
  transfers between devices with their start and end apart: 10, of which 3 were waited for; matrix products, arithmetic and copies ran while one was open for 10% of the time, Pallas kernels for 0%

commit v1 on v0

v1 whole, which is shorter than its diff:
```python
import functools

import jax
import jax.numpy as jnp
from jax import lax
from jax.experimental import pallas as pl
from jax.experimental.pallas import tpu as pltpu
from jax.sharding import Mesh
from jax.sharding import PartitionSpec as P

masked_score = -1e30
log2_e = 1.4426950408889634
row_tile = 256


def attend_kernel(plan, first, last, block_rows, shifts, queries, bias, *refs):
    arrays = refs[: plan["arrays"]]
    refs = refs[plan["arrays"] :]
    if not first:
        top_in, total_in, sum_in = refs[:3]
        refs = refs[3:]
    outs, (key_buffer, value_buffer) = refs[:-2], refs[-2:]
    slot = pl.program_id(0)

    def fill(part):
        position = 0
        for which, kind, index in plan["pieces"]:
            source = arrays[which]
            if kind == "own":
                size = source.shape[0] * 0 + source.shape[1] * source.shape[3]
                if part == "slot":
                    shape = (size, source.shape[4])
                    key_buffer[position : position + size] = source[0, :, 0].reshape(shape)
                    value_buffer[position : position + size] = source[0, :, 1].reshape(shape)
            elif kind == "extra":
                size = block_rows
                if part == "slot":
                    shift, entry = index
                    place = (slot + shifts[shift]) & 3
                    key_buffer[position : position + size] = source[place, entry, 0]
                    value_buffer[position : position + size] = source[place, entry, 1]
            else:
                size = source.shape[0] * block_rows
                if part == "once":
                    shape = (size, source.shape[4])
                    key_buffer[position : position + size] = source[:, 0, 0].reshape(shape)
                    value_buffer[position : position + size] = source[:, 0, 1].reshape(shape)
            position += size

    @pl.when((slot == 0) & (pl.program_id(1) == 0))
    def _():
        fill("once")

    @pl.when(pl.program_id(1) == 0)
    def _():
        fill("slot")

    query_tile = queries[0]
    rows, head_dim = query_tile.shape
    factor = head_dim ** (-0.5) * log2_e
    scores = lax.dot_general(
        query_tile, key_buffer[...], (((1,), (1,)), ((), ())), preferred_element_type=jnp.float32
    )
    key_count = scores.shape[1]
    scores = scores.reshape(rows // block_rows, block_rows, key_count) + bias[0, 0][:, None, :]
    scores = scores.reshape(rows, key_count)
    top = jnp.max(scores, axis=1, keepdims=True)
    if not first:
        top = jnp.maximum(top, top_in[0][:, :1])
    weights = jnp.exp2((scores - top) * factor)
    total = weights[:, :128]
    for place in range(128, key_count, 128):
        total = total + weights[:, place : place + 128]
    summed = jnp.dot(
        weights.astype(jnp.bfloat16), value_buffer[...], preferred_element_type=jnp.float32
    )
    if not first:
        shrink = jnp.exp2((top_in[0] - top) * factor)
        total = total + shrink * total_in[0]
        summed = summed + shrink * sum_in[0]
    if last:
        outs[0][0] = (summed / jnp.sum(total, axis=1, keepdims=True)).astype(jnp.bfloat16)
    else:
        outs[0][0] = jnp.broadcast_to(top, (rows, 128))
        outs[1][0] = total
        outs[2][0] = summed


def attend(queries, bias, shifts, arrays, pieces, state, last, block_rows):
    slots, slot_rows, head_dim = queries.shape
    key_count = bias.shape[-1]
    tiles = slot_rows // row_tile
    tile_spec = pl.BlockSpec((1, row_tile, head_dim), lambda s, t, *_: (s, t, 0))
    specs = [tile_spec, pl.BlockSpec((1, 1) + bias.shape[2:], lambda s, t, *_: (s, t, 0, 0))]
    for which, array in enumerate(arrays):
        own = any(kind == "own" for w, kind, index in pieces if w == which)
        if own:
            specs.append(pl.BlockSpec((1,) + array.shape[1:], lambda s, t, *_: (s, 0, 0, 0, 0)))
        else:
            specs.append(pl.BlockSpec(array.shape, lambda s, t, *_: (0, 0, 0, 0, 0)))
    state_shape = jax.ShapeDtypeStruct((slots, slot_rows, 128), jnp.float32)
    if last:
        out_shape = [jax.ShapeDtypeStruct(queries.shape, jnp.bfloat16)]
    else:
        out_shape = [state_shape] * 3
    carried = [] if state is None else list(state)
    specs += [tile_spec] * len(carried)
    plan = {"arrays": len(arrays), "pieces": pieces}
    flops = 4 * slots * slot_rows * key_count * head_dim
    return pl.pallas_call(
        functools.partial(attend_kernel, plan, state is None, last, block_rows),
        out_shape=out_shape,
        grid_spec=pltpu.PrefetchScalarGridSpec(
            num_scalar_prefetch=1,
            grid=(slots, tiles),
            in_specs=specs,
            out_specs=[tile_spec] * len(out_shape),
            scratch_shapes=[
                pltpu.VMEM((key_count, head_dim), jnp.bfloat16),
                pltpu.VMEM((key_count, head_dim), jnp.bfloat16),
            ],
        ),
        cost_estimate=pl.CostEstimate(
            flops=flops,
            transcendentals=slots * slot_rows * key_count,
            bytes_accessed=8 * 1024 * 1024,
        ),
    )(shifts, queries, bias, *arrays, *carried)


def local(queries, keys, values, block_mask, strides, offsets):
    core = lax.axis_index("core")
    depth = lax.axis_index("z")
    cores, depths, planes = lax.axis_size("core"), lax.axis_size("z"), lax.axis_size("x")
    frame_total, frame_blocks = block_mask.shape[0], block_mask.shape[1]
    local_rows, heads, head_dim = queries.shape
    rows_y = lax.axis_size("y")
    block_rows = local_rows * rows_y * cores // frame_blocks
    swap = [(0, 1), (1, 0)]
    onward = [(z, (z + 1) % depths) for z in range(depths)]
    onward += [(depths + z, depths + (z - 1) % depths) for z in range(depths)]

    packed = jnp.stack([jnp.transpose(keys, (1, 0, 2)), jnp.transpose(values, (1, 0, 2))], axis=1)
    own_pair = lax.all_to_all(packed, ("x", "y"), split_axis=0, concat_axis=0, tiled=True)
    own_pair = own_pair.reshape(planes, rows_y, 2, local_rows, head_dim)
    partner_pair = lax.ppermute(own_pair, "core", swap)
    head_queries = lax.all_to_all(
        jnp.transpose(queries, (1, 0, 2)), ("x", "y"), split_axis=0, concat_axis=0, tiled=True
    )
    head_queries = head_queries.reshape(planes, rows_y * local_rows, head_dim)

    anchors = (frame_blocks - offsets % frame_blocks) % frame_blocks
    slot_ids = jnp.arange(planes, dtype=jnp.int32)
    own_frames = slot_ids * depths + depth
    own_mask = lax.dynamic_index_in_dim(
        block_mask.reshape(planes, depths, frame_blocks, frame_blocks), depth, 1, keepdims=False
    )
    split_mask = own_mask.reshape(planes, rows_y, cores, -1, frame_blocks)
    query_mask = lax.dynamic_index_in_dim(split_mask, core, 2, keepdims=False)
    query_mask = query_mask.reshape(planes, -1, frame_blocks).astype(jnp.float32)
    signs = (2 * core - 1, 1 - 2 * core)

    def own_columns():
        shape = (rows_y, local_rows // block_rows)
        columns = []
        for side in (core, 1 - core):
            place = jnp.arange(rows_y)[:, None] * (frame_blocks // rows_y)
            place = place + side * shape[1] + jnp.arange(shape[1])[None, :]
            columns.append(jnp.broadcast_to(place.reshape(1, -1), (planes, shape[0] * shape[1])))
        columns = jnp.concatenate(columns, axis=1)
        return columns, jnp.ones(columns.shape, jnp.bool_)

    def extra_column(sign, distance, part):
        source = own_frames + sign * distance
        valid = (source >= 0) & (source < frame_total)
        column = (anchors[jnp.clip(source, 0, frame_total - 1)] + 4 * part) % frame_blocks
        kept = (4 * part) % strides[distance] == 0
        return column[:, None], (valid & kept)[:, None]

    def anchor_columns(source_depth):
        sources = slot_ids * depths + source_depth % depths
        column = jnp.broadcast_to(anchors[sources][None, :], (planes, planes))
        return column, sources[None, :] != own_frames[:, None]

    def bias_of(columns):
        column = jnp.concatenate([entry[0] for entry in columns], axis=1)
        valid = jnp.concatenate([entry[1] for entry in columns], axis=1)
        code = jnp.where(valid, column, -1).astype(jnp.int32)
        code = jnp.repeat(code, block_rows, axis=1)
        chosen = jnp.arange(frame_blocks, dtype=jnp.int32)[None, :, None] == code[:, None, :]
        kept = jnp.einsum("sbc,scn->sbn", query_mask, chosen.astype(jnp.float32))
        bias = jnp.where(kept > 0.5, 0.0, masked_score)
        tiles = rows_y * local_rows // row_tile
        return bias.reshape(planes, tiles, -1, bias.shape[-1])

    residue = anchors[own_frames] % 4
    both = jnp.stack([own_pair, partner_pair]).reshape(-1, block_rows, head_dim)
    side = (residue // 2) ^ core
    halves = local_rows // block_rows
    parts = jnp.arange(4, dtype=jnp.int32)
    row_y = (anchors[own_frames][:, None] // 4 + parts[None, :]) % 4
    index = (side[:, None] * planes + slot_ids[:, None]) * rows_y + row_y
    index = index[:, :, None] * 2 + jnp.arange(2, dtype=jnp.int32)
    index = index * halves + (residue % 2)[:, None, None]
    candidates = jnp.take(both, index.reshape(-1), axis=0).reshape(
        planes, 4, 2, block_rows, head_dim
    )

    carried = candidates
    mine, other = {}, {}
    for step in range(1, depths // 2 + 1):
        carried = lax.ppermute(carried, ("core", "z"), onward)
        mine[step] = carried
        if step < depths // 2:
            other[step] = lax.ppermute(carried, "core", swap)
        if step == 1:
            carried = jnp.stack([carried[:, 0], carried[:, 2]], axis=1)
        elif step == 3:
            carried = carried[:, :1]

    near = (1, 2, 3)
    shifts = jnp.stack([(depth + sign * k) // depths for sign in signs for k in near])
    shifts = (shifts + planes).astype(jnp.int32)

    state = attend(
        head_queries,
        bias_of([own_columns()]),
        shifts,
        [own_pair, partner_pair],
        [(0, "own", None), (1, "own", None)],
        None,
        False,
        block_rows,
    )
    arrays = [candidates[:, :1]]
    pieces = [(0, "anchor", None)]
    columns = [anchor_columns(depth)]
    for sign, held, first_shift in ((signs[0], mine, 0), (signs[1], other, 3)):
        for k in near:
            arrays.append(held[k])
            which = len(arrays) - 1
            pieces.append((which, "anchor", None))
            columns.append(anchor_columns(depth + sign * k + depths))
            for entry, part in ((1, 1), (2, 2), (3, 3)) if k == 1 else ((1, 2),):
                pieces.append((which, "extra", (first_shift + k - 1, entry)))
                columns.append(extra_column(sign, k, part))
    state = attend(
        head_queries, bias_of(columns), shifts, arrays, pieces, state, False, block_rows
    )
    for steps, last in (((4, 5, 6), False), ((7, 8), True)):
        arrays, columns = [], []
        for k in steps:
            arrays.append(mine[k])
            columns.append(anchor_columns(depth + signs[0] * k + depths))
            if k in other:
                arrays.append(other[k])
                columns.append(anchor_columns(depth + signs[1] * k + depths))
        pieces = [(which, "anchor", None) for which in range(len(arrays))]
        state = attend(
            head_queries, bias_of(columns), shifts, arrays, pieces, state, last, block_rows
        )

    output = state[0].reshape(planes * rows_y, local_rows, head_dim)
    output = lax.all_to_all(output, ("x", "y"), split_axis=0, concat_axis=0, tiled=True)
    return jnp.transpose(output, (1, 0, 2))


def solution(mesh):
    grid = Mesh(mesh.devices.reshape(4, 2, 4, 16), ("y", "core", "x", "z"))
    tokens = P(("x", "z", "y", "core"), None, None)
    return jax.shard_map(
        local,
        mesh=grid,
        in_specs=(tokens, tokens, tokens, P(), P(), P()),
        out_specs=tokens,
        check_vma=False,
    )
```

time: 513 us -> 194 us (0.38)
  local copies, waits for them, and re-layouts: 137 us -> 30.8 us
  waiting for transfers between devices: 114 us -> 11.7 us
  other arithmetic: 89 us -> 4.44 us
  matrix products: 68.6 us -> 0.7 us
  Pallas kernels: 0 us -> 44.4 us
  starting transfers between devices: 36.4 us -> 76.7 us
  between operations: 31 us -> 5.43 us
  loops' own time: 12.5 us -> 0 us
    all_gather x1 -> x0, waiting for transfers between devices: 103 us -> none  [local(): gathered = lax.all_gather(anchor_pair, 'frame', axis=0, tiled=True)]
    reduce_sum x55 -> x0, other arithmetic: 66.7 us -> none  [the longest x23 45.4 us: group_terms(): group_totals = jnp.sum(weights, axis=4)]
    ppermute x6 -> x16, starting transfers between devices: 16.9 us -> 63.7 us  [the longest x8 43.5 us: local(): carried = lax.ppermute(carried, ('core', 'z'), onward)]
    pallas_call x0 -> x4, Pallas kernels: none -> 44.4 us  [attend(): pl.pallas_call(functools.partial(attend_kernel, plan, state is None, last...]
    convert_element_type x16 -> x0, local copies, waits for them, and re-layouts: 42.6 us -> none  [group_terms(): weights.astype(jnp.bfloat16)]
    while x16 -> x0, matrix products: 36.3 us -> none
    dot_general x26 -> x4, matrix products: 30.3 us -> 0.7 us  [bias_of(): kept = jnp.einsum('sbc,scn->sbn', query_mask, chosen.astype(jnp.float32))]
    gather x58 -> x24, local copies, waits for them, and re-layouts: 35.1 us -> 15.4 us  [the longest x16 10.2 us: anchor_columns(): column = jnp.broadcast_to(anchors[sources][None, :], (planes, planes))]
  transfers between devices with their start and end apart: 10 -> 18, of which waited for: 3 -> 4; matrix products, arithmetic and copies ran while one was open for 10% -> 15% of each run, Pallas kernels for 0% -> 18%
where the time goes in v1:
time: 194 us; the launch traced here: 193 us
  starting transfers between devices  76.7 us (40%)
  Pallas kernels  44.4 us (23%)
  local copies, waits for them, and re-layouts  30.8 us (16%)
  blocking collectives  18.6 us (10%)
  waiting for transfers between devices  11.7 us (6%)
  between operations  5.43 us (3%)
  other arithmetic  4.44 us (2%)
    pallas_call x4, Pallas kernels, attend(): pl.pallas_call(functools.partial(attend_kernel, plan, state is None, last...  44.4 us
    ppermute x8, starting transfers between devices, local(): carried = lax.ppermute(carried, ('core', 'z'), onward)  43.5 us
    all_to_all x1, blocking collectives, local(): lax.all_to_all(output, ('x', 'y'), split_axis=0, concat_axis=0, tiled=True)  18.6 us
    ppermute x7, starting transfers between devices, local(): other[step] = lax.ppermute(carried, 'core', swap)  15.4 us
    gather x16, local copies, waits for them, and re-layouts, anchor_columns(): column = jnp.broadcast_to(anchors[sources][None, :], (planes, planes))  10.2 us
    ppermute x8, waiting for transfers between devices, local(): carried = lax.ppermute(carried, ('core', 'z'), onward)  9.76 us
    all_to_all x1, starting transfers between devices, local(): lax.all_to_all(packed, ('x', 'y'), split_axis=0, concat_axis=0, tiled=True)  7.57 us
    all_to_all x1, starting transfers between devices, local(): lax.all_to_all(jnp.transpose(queries, (1, 0, 2)), ('x', 'y'), split_axis=...  5.37 us
  transfers between devices with their start and end apart: 18, of which 4 were waited for; matrix products, arithmetic and copies ran while one was open for 15% of the time, Pallas kernels for 18%

profile of v1, /device:TPU:1, one launch (start us, length us, event | category | flops | bytes accessed | tf_op | source)
XLA Modules:
  0.0 192.7 jit_solution(670494593686883337)
XLA Ops:
  0.0 1.5 copy_bitcast_fusion
  1.5 1.1 pad_maximum_fusion.1
  2.6 7.6 %all-to-all-start.1 = ((bf16[16,2,128,128]{3,2,1,0:T(8,128)(2,1)}), bf16[16,2,128,128]{3,2,1,0:T(8,128)(2,1)S(1)}, u32[]{:S(2)}, u32[]{:S(2)}) async-start(bf16[16,2,128,128]{3,2,1,0:T(8,128)(2,1)} %pad_maximum_fusion.1), calls=%async_computation.1 | async-start | bytes 2097152 | tf_op jit(solution)/shard_map/all_to_all | solution.py:144
  22.7 1.9 all-to-all-done.1
  24.5 5.4 %all-to-all-start = ((bf16[16,128,128]{2,1,0:T(8,128)(2,1)}), bf16[16,128,128]{2,1,0:T(8,128)(2,1)}, u32[]{:S(2)}, u32[]{:S(2)}) async-start(bf16[16,128,128]{2,1,0:T(8,128)(2,1)} %bitcast.103), calls=%async_computation | async-start | bytes 1048576 | tf_op jit(solution)/shard_map/all_to_all | solution.py:147
  29.9 4.8 %collective-permute-start = (bf16[4,4,2,128,128]{4,3,2,1,0:T(8,128)(2,1)S(1)}, bf16[4,4,2,128,128]{4,3,2,1,0:T(8,128)(2,1)S(1)}, u32[]{:S(2)}, u32[]{:S(2)}) collective-permute-start(bf16[4,4,2,128,128]{4,3,2,1,0:T(8,128)(2,1)S(1)} %bitcast.104), channel_id=1, source_target_pairs={{0,64},{64,0},{1,65},{65,1},{2,66},{66,2},{3,67},{67,3},{4,68},{68... | collective-permute-start | bytes 3145736 | tf_op jit(solution)/shard_map/ppermute | solution.py:146
  46.6 1.0 copy-done.1
  47.5 1.4 pad_maximum_fusion
  49.7 11.5 %collective-permute-start.1 = (bf16[4,4,2,64,128]{4,3,2,1,0:T(8,128)(2,1)S(1)}, bf16[4,4,2,64,128]{4,3,2,1,0:T(8,128)(2,1)S(1)}, u32[]{:S(2)}, u32[]{:S(2)}) collective-permute-start(bf16[4,4,2,64,128]{4,3,2,1,0:T(8,128)(2,1)S(1)} %broadcast_select_fusion), channel_id=1, source_target_pairs={{0,1},{1,2},{2,3},{3,4},{4,5},{5,6},{6,7},{7,8},{8,9},{9,10},{10,1... | collective-permute-start | bytes 1572872 | tf_op jit(solution)/shard_map/ppermute | solution.py:212
  61.4 5.9 %collective-permute-done.1.refs_1_ = bf16[4,4,2,64,128]{4,3,2,1,0:T(8,128)(2,1)S(1)} collective-permute-done((bf16[4,4,2,64,128]{4,3,2,1,0:T(8,128)(2,1)S(1)}, bf16[4,4,2,64,128]{4,3,2,1,0:T(8,128)(2,1)S(1)}, u32[]{:S(2)}, u32[]{:S(2)}) %collective-permute-start.1) | collective-permute-done | bytes 524320 | tf_op jit(solution)/shard_map/ppermute | solution.py:212
  67.4 5.0 %collective-permute-start.2 = (bf16[4,2,2,64,128]{4,3,2,1,0:T(8,128)(2,1)S(1)}, bf16[4,2,2,64,128]{4,3,2,1,0:T(8,128)(2,1)S(1)}, u32[]{:S(2)}, u32[]{:S(2)}) collective-permute-start(bf16[4,2,2,64,128]{4,3,2,1,0:T(8,128)(2,1)S(1)} %pad_maximum_fusion.2), channel_id=1, source_target_pairs={{0,1},{1,2},{2,3},{3,4},{4,5},{5,6},{6,7},{7,8},{8,9},{9,10},{10,1... | collective-permute-start | bytes 786440 | tf_op jit(solution)/shard_map/ppermute | solution.py:212
  74.7 1.0 collective-permute-done.2.refs_2_
  75.7 5.0 %collective-permute-start.3 = (bf16[4,2,2,64,128]{4,3,2,1,0:T(8,128)(2,1)S(1)}, bf16[4,2,2,64,128]{4,3,2,1,0:T(8,128)(2,1)S(1)}, u32[]{:S(2)}, u32[]{:S(2)}) collective-permute-start(bf16[4,2,2,64,128]{4,3,2,1,0:T(8,128)(2,1)S(1)} %collective-permute-done.2.refs_2_), channel_id=1, source_target_pairs={{0,1},{1,2},{2,3},{3,4},{4,5},{5,6},{6,7},{7,8},{8,9},{9,10},{10,1... | collective-permute-start | bytes 786440 | tf_op jit(solution)/shard_map/ppermute | solution.py:212
  81.2 2.8 %collective-permute-done.3.refs_3_ = bf16[4,2,2,64,128]{4,3,2,1,0:T(8,128)(2,1)S(1)} collective-permute-done((bf16[4,2,2,64,128]{4,3,2,1,0:T(8,128)(2,1)S(1)}, bf16[4,2,2,64,128]{4,3,2,1,0:T(8,128)(2,1)S(1)}, u32[]{:S(2)}, u32[]{:S(2)}) %collective-permute-start.3) | collective-permute-done | bytes 262176 | tf_op jit(solution)/shard_map/ppermute | solution.py:212
  84.0 5.0 %collective-permute-start.4 = (bf16[4,1,2,64,128]{4,3,2,1,0:T(8,128)(2,1)S(1)}, bf16[4,1,2,64,128]{4,3,2,1,0:T(8,128)(2,1)}, u32[]{:S(2)}, u32[]{:S(2)}) collective-permute-start(bf16[4,1,2,64,128]{4,3,2,1,0:T(8,128)(2,1)S(1)} %slice.85), channel_id=1, source_target_pairs={{0,1},{1,2},{2,3},{3,4},{4,5},{5,6},{6,7},{7,8},{8,9},{9,10},{10,1... | collective-permute-start | bytes 393224 | tf_op jit(solution)/shard_map/ppermute | solution.py:212
  89.5 2.4 %collective-permute-start.13 = (bf16[4,4,2,64,128]{4,3,2,1,0:T(8,128)(2,1)S(1)}, bf16[4,4,2,64,128]{4,3,2,1,0:T(8,128)(2,1)S(1)}, u32[]{:S(2)}, u32[]{:S(2)}) collective-permute-start(bf16[4,4,2,64,128]{4,3,2,1,0:T(8,128)(2,1)S(1)} %collective-permute-done.1.refs_1_), channel_id=1, source_target_pairs={{0,64},{64,0},{1,65},{65,1},{2,66},{66,2},{3,67},{67,3},{4,68},{68... | collective-permute-start | bytes 1572872 | tf_op jit(solution)/shard_map/ppermute | solution.py:215
  91.9 4.9 %collective-permute-start.5 = (bf16[4,1,2,64,128]{4,3,2,1,0:T(8,128)(2,1)}, bf16[4,1,2,64,128]{4,3,2,1,0:T(8,128)(2,1)}, u32[]{:S(2)}, u32[]{:S(2)}) collective-permute-start(bf16[4,1,2,64,128]{4,3,2,1,0:T(8,128)(2,1)} %collective-permute-done.4.refs_0_), channel_id=1, source_target_pairs={{0,1},{1,2},{2,3},{3,4},{4,5},{5,6},{6,7},{7,8},{8,9},{9,10},{10,1... | collective-permute-start | bytes 393224 | tf_op jit(solution)/shard_map/ppermute | solution.py:212
  96.9 2.9 %collective-permute-start.14 = (bf16[4,2,2,64,128]{4,3,2,1,0:T(8,128)(2,1)S(1)}, bf16[4,2,2,64,128]{4,3,2,1,0:T(8,128)(2,1)S(1)}, u32[]{:S(2)}, u32[]{:S(2)}) collective-permute-start(bf16[4,2,2,64,128]{4,3,2,1,0:T(8,128)(2,1)S(1)} %collective-permute-done.2.refs_2_), channel_id=1, source_target_pairs={{0,64},{64,0},{1,65},{65,1},{2,66},{66,2},{3,67},{67,3},{4,68},{68... | collective-permute-start | bytes 786440 | tf_op jit(solution)/shard_map/ppermute | solution.py:215
  99.8 1.9 collective-permute-start.15
  101.8 4.9 %collective-permute-start.6 = (bf16[4,1,2,64,128]{4,3,2,1,0:T(8,128)(2,1)}, bf16[4,1,2,64,128]{4,3,2,1,0:T(8,128)(2,1)}, u32[]{:S(2)}, u32[]{:S(2)}) collective-permute-start(bf16[4,1,2,64,128]{4,3,2,1,0:T(8,128)(2,1)} %collective-permute-done.5.refs_2_), channel_id=1, source_target_pairs={{0,1},{1,2},{2,3},{3,4},{4,5},{5,6},{6,7},{7,8},{8,9},{9,10},{10,1... | collective-permute-start | bytes 393224 | tf_op jit(solution)/shard_map/ppermute | solution.py:212
  110.8 9.1 %shard_map.64 = (f32[4,512,128]{2,1,0:T(8,128)}, f32[4,512,128]{2,1,0:T(8,128)}, f32[4,512,128]{2,1,0:T(8,128)}) custom-call(s32[6]{0:T(128)} %broadcast_add_fusion.shifts, bf16[4,512,128]{2,1,0:T(8,128)(2,1)} %bitcast.7.queries, f32[4,2,4,1024]{3,2,1,0:T(4,128)} %reshape.1196.bias, bf16[4,4,2,128,128]{4,3,2,1,0:T(8,128)(2,1)} %bitcast.106, ...), custom_call_target="tpu_custom_call" | custom-call | flops 1073741824 | bytes 8388608 | tf_op jit(solution)/shard_map/pallas_call | solution.py:110
  119.9 1.9 collective-permute-start.10
  121.9 2.4 %collective-permute-start.11 = (bf16[4,1,2,64,128]{4,3,2,1,0:T(8,128)(2,1)}, bf16[4,1,2,64,128]{4,3,2,1,0:T(8,128)(2,1)S(1)}, u32[]{:S(2)}, u32[]{:S(2)}) collective-permute-start(bf16[4,1,2,64,128]{4,3,2,1,0:T(8,128)(2,1)} %collective-permute-done.5.refs_2_), channel_id=1, source_target_pairs={{0,64},{64,0},{1,65},{65,1},{2,66},{66,2},{3,67},{67,3},{4,68},{68... | collective-permute-start | bytes 393224 | tf_op jit(solution)/shard_map/ppermute | solution.py:215
  124.3 1.9 collective-permute-start.12
  126.2 4.4 %collective-permute-start.7 = (bf16[4,1,2,64,128]{4,3,2,1,0:T(8,128)(2,1)}, bf16[4,1,2,64,128]{4,3,2,1,0:T(8,128)(2,1)S(1)}, u32[]{:S(2)}, u32[]{:S(2)}) collective-permute-start(bf16[4,1,2,64,128]{4,3,2,1,0:T(8,128)(2,1)} %collective-permute-done.6.refs_4_), channel_id=1, source_target_pairs={{0,1},{1,2},{2,3},{3,4},{4,5},{5,6},{6,7},{7,8},{8,9},{9,10},{10,1... | collective-permute-start | bytes 393224 | tf_op jit(solution)/shard_map/ppermute | solution.py:212
  131.3 14.3 %shard_map.65 = (f32[4,512,128]{2,1,0:T(8,128)}, f32[4,512,128]{2,1,0:T(8,128)}, f32[4,512,128]{2,1,0:T(8,128)}) custom-call(s32[6]{0:T(128)} %broadcast_add_fusion.shifts, bf16[4,512,128]{2,1,0:T(8,128)(2,1)} %bitcast.7.queries, f32[4,2,4,2432]{3,2,1,0:T(4,128)} %reshape.1195.bias, bf16[4,1,2,64,128]{4,3,2,1,0:T(8,128)(2,1)} %slice.86.refs_0_, ...), custom_call_target="tpu_custom_call" | custom-call | flops 2550136832 | bytes 8388608 | tf_op jit(solution)/shard_map/pallas_call | solution.py:110
  145.6 1.9 collective-permute-start.8
  147.6 2.9 %collective-permute-start.9 = (bf16[4,1,2,64,128]{4,3,2,1,0:T(8,128)(2,1)S(1)}, bf16[4,1,2,64,128]{4,3,2,1,0:T(8,128)(2,1)S(1)}, u32[]{:S(2)}, u32[]{:S(2)}) collective-permute-start(bf16[4,1,2,64,128]{4,3,2,1,0:T(8,128)(2,1)S(1)} %collective-permute-done.7.refs_0_), channel_id=1, source_target_pairs={{0,1},{1,2},{2,3},{3,4},{4,5},{5,6},{6,7},{7,8},{8,9},{9,10},{10,1... | collective-permute-start | bytes 393224 | tf_op jit(solution)/shard_map/ppermute | solution.py:212
  151.2 11.2 %shard_map.66 = (f32[4,512,128]{2,1,0:T(8,128)}, f32[4,512,128]{2,1,0:T(8,128)}, f32[4,512,128]{2,1,0:T(8,128)}) custom-call(s32[6]{0:T(128)} %broadcast_add_fusion.shifts, bf16[4,512,128]{2,1,0:T(8,128)(2,1)} %bitcast.7.queries, f32[4,2,4,1536]{3,2,1,0:T(4,128)} %reshape.1194.bias, bf16[4,1,2,64,128]{4,3,2,1,0:T(8,128)(2,1)} %collective-permute-done.4.refs_0_, ...), custom_call_target="tpu_custom_call" | custom-call | flops 1610612736 | bytes 8388608 | tf_op jit(solution)/shard_map/pallas_call | solution.py:110
  163.1 9.9 %shard_map.67 = bf16[4,512,128]{2,1,0:T(8,128)(2,1)} custom-call(s32[6]{0:T(128)} %broadcast_add_fusion.shifts, bf16[4,512,128]{2,1,0:T(8,128)(2,1)} %bitcast.7.queries, f32[4,2,4,768]{3,2,1,0:T(4,128)} %reshape.1191.bias, bf16[4,1,2,64,128]{4,3,2,1,0:T(8,128)(2,1)} %copy-done.4, bf16[4,1,2,64,128]{4,3,2,1,0:T(8,128)(2,1)} %copy-done.5, ...), custom_call_target="tpu_custom_call" | custom-call | flops 805306368 | bytes 8388608 | tf_op jit(solution)/shard_map/pallas_call | solution.py:110
  173.0 18.6 %all_to_all.15 = bf16[16,128,128]{2,1,0:T(8,128)(2,1)S(1)} all-to-all(bf16[16,128,128]{2,1,0:T(8,128)(2,1)} %bitcast.108), channel_id=1, replica_groups=mesh['y'=4,'core'=2,'x'=4,'z'=16] {'x','y'}, dimensions={0} | all-to-all | bytes 1048576 | tf_op jit(solution)/shard_map/all_to_all | solution.py:264
  191.6 1.1 copy.104
  (216 shorter events, 29.8 us)
Async XLA Ops:
  1.5 8.9 %copy-start.9 = (s32[64]{0:T(128)S(1)}, s32[64]{0:T(128)}, u32[]{:S(2)}) copy-start(s32[64]{0:T(128)} %param.10) | copy-start | bytes 772
  1.5 14.2 %copy-start.17 = (s32[64]{0:T(128)S(1)}, s32[64]{0:T(128)}, u32[]{:S(2)}) copy-start(s32[64]{0:T(128)} %param.11) | copy-start | bytes 772
  2.6 21.9 %all-to-all-start.1 = ((bf16[16,2,128,128]{3,2,1,0:T(8,128)(2,1)}), bf16[16,2,128,128]{3,2,1,0:T(8,128)(2,1)S(1)}, u32[]{:S(2)}, u32[]{:S(2)}) async-start(bf16[16,2,128,128]{3,2,1,0:T(8,128)(2,1)} %pad_maximum_fusion.1), calls=%async_computation.1 | async-start | bytes 2097152 | tf_op jit(solution)/shard_map/all_to_all | solution.py:144
  10.2 9.5 %copy-start.3 = (s32[64,16,16]{0,2,1:T(8,128)S(1)}, s32[64,16,16]{0,2,1:T(8,128)}, u32[]{:S(2)}) copy-start(s32[64,16,16]{0,2,1:T(8,128)} %param.9) | copy-start | bytes 196612
  10.4 9.9 %copy-start.2 = (bf16[128,16,128]{2,1,0:T(8,128)(2,1)S(1)}, bf16[128,16,128]{2,1,0:T(8,128)(2,1)}, u32[]{:S(2)}) copy-start(bf16[128,16,128]{2,1,0:T(8,128)(2,1)} %param.6) | copy-start | bytes 1572868
  24.5 23.0 %copy-start = (bf16[16,2,128,128]{3,2,1,0:T(8,128)(2,1)}, bf16[16,2,128,128]{3,2,1,0:T(8,128)(2,1)S(1)}, u32[]{:S(2)}) copy-start(bf16[16,2,128,128]{3,2,1,0:T(8,128)(2,1)S(1)} %all-to-all-done.1) | copy-start | bytes 3145732
  24.5 86.3 %all-to-all-start = ((bf16[16,128,128]{2,1,0:T(8,128)(2,1)}), bf16[16,128,128]{2,1,0:T(8,128)(2,1)}, u32[]{:S(2)}, u32[]{:S(2)}) async-start(bf16[16,128,128]{2,1,0:T(8,128)(2,1)} %bitcast.103), calls=%async_computation | async-start | bytes 1048576 | tf_op jit(solution)/shard_map/all_to_all | solution.py:147
  29.9 16.6 %collective-permute-start = (bf16[4,4,2,128,128]{4,3,2,1,0:T(8,128)(2,1)S(1)}, bf16[4,4,2,128,128]{4,3,2,1,0:T(8,128)(2,1)S(1)}, u32[]{:S(2)}, u32[]{:S(2)}) collective-permute-start(bf16[4,4,2,128,128]{4,3,2,1,0:T(8,128)(2,1)S(1)} %bitcast.104), channel_id=1, source_target_pairs={{0,64},{64,0},{1,65},{65,1},{2,66},{66,2},{3,67},{67,3},{4,68},{68... | collective-permute-start | bytes 3145736 | tf_op jit(solution)/shard_map/ppermute | solution.py:146
  46.6 1.0 copy-start.1
  49.7 17.6 %collective-permute-start.1 = (bf16[4,4,2,64,128]{4,3,2,1,0:T(8,128)(2,1)S(1)}, bf16[4,4,2,64,128]{4,3,2,1,0:T(8,128)(2,1)S(1)}, u32[]{:S(2)}, u32[]{:S(2)}) collective-permute-start(bf16[4,4,2,64,128]{4,3,2,1,0:T(8,128)(2,1)S(1)} %broadcast_select_fusion), channel_id=1, source_target_pairs={{0,1},{1,2},{2,3},{3,4},{4,5},{5,6},{6,7},{7,8},{8,9},{9,10},{10,1... | collective-permute-start | bytes 1572872 | tf_op jit(solution)/shard_map/ppermute | solution.py:212
  67.3 29.6 %copy-start.7 = (bf16[4,4,2,64,128]{4,3,2,1,0:T(8,128)(2,1)}, bf16[4,4,2,64,128]{4,3,2,1,0:T(8,128)(2,1)S(1)}, u32[]{:S(2)}) copy-start(bf16[4,4,2,64,128]{4,3,2,1,0:T(8,128)(2,1)S(1)} %collective-permute-done.1.refs_1_) | copy-start | bytes 1572868
  67.4 8.3 %collective-permute-start.2 = (bf16[4,2,2,64,128]{4,3,2,1,0:T(8,128)(2,1)S(1)}, bf16[4,2,2,64,128]{4,3,2,1,0:T(8,128)(2,1)S(1)}, u32[]{:S(2)}, u32[]{:S(2)}) collective-permute-start(bf16[4,2,2,64,128]{4,3,2,1,0:T(8,128)(2,1)S(1)} %pad_maximum_fusion.2), channel_id=1, source_target_pairs={{0,1},{1,2},{2,3},{3,4},{4,5},{5,6},{6,7},{7,8},{8,9},{9,10},{10,1... | collective-permute-start | bytes 786440 | tf_op jit(solution)/shard_map/ppermute | solution.py:212
  75.7 44.2 %copy-start.11 = (bf16[4,2,2,64,128]{4,3,2,1,0:T(8,128)(2,1)}, bf16[4,2,2,64,128]{4,3,2,1,0:T(8,128)(2,1)S(1)}, u32[]{:S(2)}) copy-start(bf16[4,2,2,64,128]{4,3,2,1,0:T(8,128)(2,1)S(1)} %collective-permute-done.2.refs_2_) | copy-start | bytes 786436
  75.7 8.3 %collective-permute-start.3 = (bf16[4,2,2,64,128]{4,3,2,1,0:T(8,128)(2,1)S(1)}, bf16[4,2,2,64,128]{4,3,2,1,0:T(8,128)(2,1)S(1)}, u32[]{:S(2)}, u32[]{:S(2)}) collective-permute-start(bf16[4,2,2,64,128]{4,3,2,1,0:T(8,128)(2,1)S(1)} %collective-permute-done.2.refs_2_), channel_id=1, source_target_pairs={{0,1},{1,2},{2,3},{3,4},{4,5},{5,6},{6,7},{7,8},{8,9},{9,10},{10,1... | collective-permute-start | bytes 786440 | tf_op jit(solution)/shard_map/ppermute | solution.py:212
  84.0 35.9 %copy-start.8 = (bf16[4,2,2,64,128]{4,3,2,1,0:T(8,128)(2,1)}, bf16[4,2,2,64,128]{4,3,2,1,0:T(8,128)(2,1)S(1)}, u32[]{:S(2)}) copy-start(bf16[4,2,2,64,128]{4,3,2,1,0:T(8,128)(2,1)S(1)} %collective-permute-done.3.refs_3_) | copy-start | bytes 786436
  84.0 7.9 %collective-permute-start.4 = (bf16[4,1,2,64,128]{4,3,2,1,0:T(8,128)(2,1)S(1)}, bf16[4,1,2,64,128]{4,3,2,1,0:T(8,128)(2,1)}, u32[]{:S(2)}, u32[]{:S(2)}) collective-permute-start(bf16[4,1,2,64,128]{4,3,2,1,0:T(8,128)(2,1)S(1)} %slice.85), channel_id=1, source_target_pairs={{0,1},{1,2},{2,3},{3,4},{4,5},{5,6},{6,7},{7,8},{8,9},{9,10},{10,1... | collective-permute-start | bytes 393224 | tf_op jit(solution)/shard_map/ppermute | solution.py:212
  89.5 36.8 %collective-permute-start.13 = (bf16[4,4,2,64,128]{4,3,2,1,0:T(8,128)(2,1)S(1)}, bf16[4,4,2,64,128]{4,3,2,1,0:T(8,128)(2,1)S(1)}, u32[]{:S(2)}, u32[]{:S(2)}) collective-permute-start(bf16[4,4,2,64,128]{4,3,2,1,0:T(8,128)(2,1)S(1)} %collective-permute-done.1.refs_1_), channel_id=1, source_target_pairs={{0,64},{64,0},{1,65},{65,1},{2,66},{66,2},{3,67},{67,3},{4,68},{68... | collective-permute-start | bytes 1572872 | tf_op jit(solution)/shard_map/ppermute | solution.py:215
  91.9 9.9 %collective-permute-start.5 = (bf16[4,1,2,64,128]{4,3,2,1,0:T(8,128)(2,1)}, bf16[4,1,2,64,128]{4,3,2,1,0:T(8,128)(2,1)}, u32[]{:S(2)}, u32[]{:S(2)}) collective-permute-start(bf16[4,1,2,64,128]{4,3,2,1,0:T(8,128)(2,1)} %collective-permute-done.4.refs_0_), channel_id=1, source_target_pairs={{0,1},{1,2},{2,3},{3,4},{4,5},{5,6},{6,7},{7,8},{8,9},{9,10},{10,1... | collective-permute-start | bytes 393224 | tf_op jit(solution)/shard_map/ppermute | solution.py:212
  96.9 24.9 %collective-permute-start.14 = (bf16[4,2,2,64,128]{4,3,2,1,0:T(8,128)(2,1)S(1)}, bf16[4,2,2,64,128]{4,3,2,1,0:T(8,128)(2,1)S(1)}, u32[]{:S(2)}, u32[]{:S(2)}) collective-permute-start(bf16[4,2,2,64,128]{4,3,2,1,0:T(8,128)(2,1)S(1)} %collective-permute-done.2.refs_2_), channel_id=1, source_target_pairs={{0,64},{64,0},{1,65},{65,1},{2,66},{66,2},{3,67},{67,3},{4,68},{68... | collective-permute-start | bytes 786440 | tf_op jit(solution)/shard_map/ppermute | solution.py:215
  99.8 30.8 %collective-permute-start.15 = (bf16[4,2,2,64,128]{4,3,2,1,0:T(8,128)(2,1)S(1)}, bf16[4,2,2,64,128]{4,3,2,1,0:T(8,128)(2,1)S(1)}, u32[]{:S(2)}, u32[]{:S(2)}) collective-permute-start(bf16[4,2,2,64,128]{4,3,2,1,0:T(8,128)(2,1)S(1)} %collective-permute-done.3.refs_3_), channel_id=1, source_target_pairs={{0,64},{64,0},{1,65},{65,1},{2,66},{66,2},{3,67},{67,3},{4,68},{68... | collective-permute-start | bytes 786440 | tf_op jit(solution)/shard_map/ppermute | solution.py:215
  101.8 22.5 %collective-permute-start.6 = (bf16[4,1,2,64,128]{4,3,2,1,0:T(8,128)(2,1)}, bf16[4,1,2,64,128]{4,3,2,1,0:T(8,128)(2,1)}, u32[]{:S(2)}, u32[]{:S(2)}) collective-permute-start(bf16[4,1,2,64,128]{4,3,2,1,0:T(8,128)(2,1)} %collective-permute-done.5.refs_2_), channel_id=1, source_target_pairs={{0,1},{1,2},{2,3},{3,4},{4,5},{5,6},{6,7},{7,8},{8,9},{9,10},{10,1... | collective-permute-start | bytes 393224 | tf_op jit(solution)/shard_map/ppermute | solution.py:212
  119.9 30.5 %collective-permute-start.10 = (bf16[4,1,2,64,128]{4,3,2,1,0:T(8,128)(2,1)}, bf16[4,1,2,64,128]{4,3,2,1,0:T(8,128)(2,1)S(1)}, u32[]{:S(2)}, u32[]{:S(2)}) collective-permute-start(bf16[4,1,2,64,128]{4,3,2,1,0:T(8,128)(2,1)} %collective-permute-done.4.refs_0_), channel_id=1, source_target_pairs={{0,64},{64,0},{1,65},{65,1},{2,66},{66,2},{3,67},{67,3},{4,68},{68... | collective-permute-start | bytes 393224 | tf_op jit(solution)/shard_map/ppermute | solution.py:215
  121.9 8.8 %copy-start.12 = (bf16[4,2,2,64,128]{4,3,2,1,0:T(8,128)(2,1)}, bf16[4,2,2,64,128]{4,3,2,1,0:T(8,128)(2,1)S(1)}, u32[]{:S(2)}) copy-start(bf16[4,2,2,64,128]{4,3,2,1,0:T(8,128)(2,1)S(1)} %collective-permute-done.14.refs_5_) | copy-start | bytes 786436
  121.9 28.6 %collective-permute-start.11 = (bf16[4,1,2,64,128]{4,3,2,1,0:T(8,128)(2,1)}, bf16[4,1,2,64,128]{4,3,2,1,0:T(8,128)(2,1)S(1)}, u32[]{:S(2)}, u32[]{:S(2)}) collective-permute-start(bf16[4,1,2,64,128]{4,3,2,1,0:T(8,128)(2,1)} %collective-permute-done.5.refs_2_), channel_id=1, source_target_pairs={{0,64},{64,0},{1,65},{65,1},{2,66},{66,2},{3,67},{67,3},{4,68},{68... | collective-permute-start | bytes 393224 | tf_op jit(solution)/shard_map/ppermute | solution.py:215
  124.3 26.2 %collective-permute-start.12 = (bf16[4,1,2,64,128]{4,3,2,1,0:T(8,128)(2,1)}, bf16[4,1,2,64,128]{4,3,2,1,0:T(8,128)(2,1)S(1)}, u32[]{:S(2)}, u32[]{:S(2)}) collective-permute-start(bf16[4,1,2,64,128]{4,3,2,1,0:T(8,128)(2,1)} %collective-permute-done.6.refs_4_), channel_id=1, source_target_pairs={{0,64},{64,0},{1,65},{65,1},{2,66},{66,2},{3,67},{67,3},{4,68},{68... | collective-permute-start | bytes 393224 | tf_op jit(solution)/shard_map/ppermute | solution.py:215
  126.2 4.4 %copy-start.10 = (bf16[4,4,2,64,128]{4,3,2,1,0:T(8,128)(2,1)}, bf16[4,4,2,64,128]{4,3,2,1,0:T(8,128)(2,1)S(1)}, u32[]{:S(2)}) copy-start(bf16[4,4,2,64,128]{4,3,2,1,0:T(8,128)(2,1)S(1)} %collective-permute-done.13.refs_4_) | copy-start | bytes 1572868
  126.2 19.4 %collective-permute-start.7 = (bf16[4,1,2,64,128]{4,3,2,1,0:T(8,128)(2,1)}, bf16[4,1,2,64,128]{4,3,2,1,0:T(8,128)(2,1)S(1)}, u32[]{:S(2)}, u32[]{:S(2)}) collective-permute-start(bf16[4,1,2,64,128]{4,3,2,1,0:T(8,128)(2,1)} %collective-permute-done.6.refs_4_), channel_id=1, source_target_pairs={{0,1},{1,2},{2,3},{3,4},{4,5},{5,6},{6,7},{7,8},{8,9},{9,10},{10,1... | collective-permute-start | bytes 393224 | tf_op jit(solution)/shard_map/ppermute | solution.py:212
  130.6 0.7 copy-start.13
  145.6 16.8 %copy-start.4 = (bf16[4,1,2,64,128]{4,3,2,1,0:T(8,128)(2,1)}, bf16[4,1,2,64,128]{4,3,2,1,0:T(8,128)(2,1)S(1)}, u32[]{:S(2)}) copy-start(bf16[4,1,2,64,128]{4,3,2,1,0:T(8,128)(2,1)S(1)} %collective-permute-done.7.refs_0_) | copy-start | bytes 393220
  145.6 16.8 %collective-permute-start.8 = (bf16[4,1,2,64,128]{4,3,2,1,0:T(8,128)(2,1)S(1)}, bf16[4,1,2,64,128]{4,3,2,1,0:T(8,128)(2,1)S(1)}, u32[]{:S(2)}, u32[]{:S(2)}) collective-permute-start(bf16[4,1,2,64,128]{4,3,2,1,0:T(8,128)(2,1)S(1)} %collective-permute-done.7.refs_0_), channel_id=1, source_target_pairs={{0,64},{64,0},{1,65},{65,1},{2,66},{66,2},{3,67},{67,3},{4,68},{68... | collective-permute-start | bytes 393224 | tf_op jit(solution)/shard_map/ppermute | solution.py:215
  147.6 14.9 %collective-permute-start.9 = (bf16[4,1,2,64,128]{4,3,2,1,0:T(8,128)(2,1)S(1)}, bf16[4,1,2,64,128]{4,3,2,1,0:T(8,128)(2,1)S(1)}, u32[]{:S(2)}, u32[]{:S(2)}) collective-permute-start(bf16[4,1,2,64,128]{4,3,2,1,0:T(8,128)(2,1)S(1)} %collective-permute-done.7.refs_0_), channel_id=1, source_target_pairs={{0,1},{1,2},{2,3},{3,4},{4,5},{5,6},{6,7},{7,8},{8,9},{9,10},{10,1... | collective-permute-start | bytes 393224 | tf_op jit(solution)/shard_map/ppermute | solution.py:212
  150.5 0.7 copy-start.16
  (4 other events, 2.7 us)

commit v2 on v1

v2 whole, which is shorter than its diff:
```python
import functools

import jax
import jax.numpy as jnp
import numpy as np
from jax import lax
from jax.experimental import pallas as pl
from jax.experimental.pallas import tpu as pltpu
from jax.sharding import Mesh
from jax.sharding import PartitionSpec as P


masked_score = -1e30
log2_e = 1.4426950408889634
row_tile = 256


def attend_kernel(plan, first, last, block_rows, shifts, queries, bias, *refs):
    arrays = refs[: plan["arrays"]]
    refs = refs[plan["arrays"] :]
    if not first:
        marks_in, sum_in = refs[:2]
        refs = refs[2:]
    outs, (key_buffer, value_buffer, score_buffer) = refs[:-3], refs[-3:]
    slot = pl.program_id(0)

    def fill(part):
        position = 0
        for which, kind, index in plan["pieces"]:
            source = arrays[which]
            head_dim = source.shape[4]
            if kind == "own":
                size = source.shape[1] * source.shape[3]
                if part == "slot":
                    shape = (size, head_dim)
                    key_buffer[position : position + size] = source[0, :, 0].reshape(shape)
                    value_buffer[position : position + size] = source[0, :, 1].reshape(shape)
            elif kind == "extra":
                size = block_rows
                if part == "slot":
                    shift, entry = index
                    place = (slot + shifts[shift]) & 3
                    key_buffer[position : position + size] = source[place, entry, 0]
                    value_buffer[position : position + size] = source[place, entry, 1]
            else:
                size = source.shape[0] * block_rows
                if part == "once":
                    shape = (size, head_dim)
                    key_buffer[position : position + size] = source[:, index, 0].reshape(shape)
                    value_buffer[position : position + size] = source[:, index, 1].reshape(shape)
            position += size
        spare = key_buffer.shape[0] - position
        if part == "once" and spare:
            key_buffer[position:] = jnp.zeros((spare, key_buffer.shape[1]), jnp.bfloat16)
            value_buffer[position:] = jnp.zeros((spare, key_buffer.shape[1]), jnp.bfloat16)

    @pl.when(slot == 0)
    def _():
        fill("once")

    if any(kind != "anchor" for _, kind, _ in plan["pieces"]):
        fill("slot")

    key_count, head_dim = key_buffer.shape
    factor = head_dim ** (-0.5) * log2_e
    groups = row_tile // block_rows
    chunks = [(at, min(256, key_count - at)) for at in range(0, key_count, 256)]

    for tile in range(queries.shape[1] // row_tile):
        rows = slice(tile * row_tile, (tile + 1) * row_tile)
        query_tile = queries[0, rows]
        highest = None
        for at, width in chunks:
            scores = lax.dot_general(
                query_tile,
                key_buffer[at : at + width],
                (((1,), (1,)), ((), ())),
                preferred_element_type=jnp.float32,
            )
            seen = bias[0, tile * groups : (tile + 1) * groups, at : at + width]
            scores = scores.reshape(groups, block_rows, width) + seen[:, None, :]
            scores = scores.reshape(row_tile, width)
            score_buffer[:, at : at + width] = scores
            for place in range(0, width, 128):
                part = scores[:, place : place + 128]
                highest = part if highest is None else jnp.maximum(highest, part)
        top = jnp.max(highest, axis=1, keepdims=True)
        if not first:
            top = jnp.maximum(top, marks_in[0, rows, :1])
        total = jnp.zeros((row_tile, 128), jnp.float32)
        summed = jnp.zeros((row_tile, head_dim), jnp.float32)
        for at, width in chunks:
            weights = jnp.exp2((score_buffer[:, at : at + width] - top) * factor)
            for place in range(0, width, 128):
                total = total + weights[:, place : place + 128]
            summed = summed + jnp.dot(
                weights.astype(jnp.bfloat16),
                value_buffer[at : at + width],
                preferred_element_type=jnp.float32,
            )
        total = jnp.sum(total, axis=1, keepdims=True)
        if not first:
            shrink = jnp.exp2((marks_in[0, rows, :1] - top) * factor)
            total = total + shrink * marks_in[0, rows, 127:]
            summed = summed + shrink * sum_in[0, rows]
        if last:
            outs[0][0, rows] = (summed / total).astype(jnp.bfloat16)
        else:
            lane = lax.broadcasted_iota(jnp.int32, (row_tile, 128), 1)
            outs[0][0, rows] = jnp.where(lane < 64, top, total)
            outs[1][0, rows] = summed


def attend(queries, bias, shifts, arrays, pieces, state, last, block_rows):
    slots, slot_rows, head_dim = queries.shape
    key_count = bias.shape[-1]
    slot_spec = pl.BlockSpec((1, slot_rows, head_dim), lambda s, *_: (s, 0, 0))
    specs = [slot_spec, pl.BlockSpec((1,) + bias.shape[1:], lambda s, *_: (s, 0, 0))]
    for which, array in enumerate(arrays):
        own = any(kind == "own" for w, kind, index in pieces if w == which)
        if own:
            specs.append(pl.BlockSpec((1,) + array.shape[1:], lambda s, *_: (s, 0, 0, 0, 0)))
        else:
            specs.append(pl.BlockSpec(array.shape, lambda s, *_: (0, 0, 0, 0, 0)))
    state_shape = jax.ShapeDtypeStruct((slots, slot_rows, 128), jnp.float32)
    if last:
        out_shape = [jax.ShapeDtypeStruct(queries.shape, jnp.bfloat16)]
    else:
        out_shape = [state_shape] * 2
    carried = [] if state is None else list(state)
    specs += [slot_spec] * len(carried)
    plan = {"arrays": len(arrays), "pieces": pieces}
    return pl.pallas_call(
        functools.partial(attend_kernel, plan, state is None, last, block_rows),
        out_shape=out_shape,
        grid_spec=pltpu.PrefetchScalarGridSpec(
            num_scalar_prefetch=1,
            grid=(slots,),
            in_specs=specs,
            out_specs=[slot_spec] * len(out_shape),
            scratch_shapes=[
                pltpu.VMEM((key_count, head_dim), jnp.bfloat16),
                pltpu.VMEM((key_count, head_dim), jnp.bfloat16),
                pltpu.VMEM((row_tile, key_count), jnp.float32),
            ],
        ),
        cost_estimate=pl.CostEstimate(
            flops=4 * slots * slot_rows * key_count * head_dim,
            transcendentals=slots * slot_rows * key_count,
            bytes_accessed=8 * 1024 * 1024,
        ),
    )(shifts, queries, bias, *arrays, *carried)


def after(value, *earlier):
    return lax.optimization_barrier((value,) + earlier)[0]


def local(queries, keys, values, block_mask, strides, offsets):
    core = lax.axis_index("core")
    plane = lax.axis_index("x")
    depth = lax.axis_index("z")
    cores, depths, planes = lax.axis_size("core"), lax.axis_size("z"), lax.axis_size("x")
    frame_total, frame_blocks = block_mask.shape[0], block_mask.shape[1]
    local_rows, _, head_dim = queries.shape
    rows_y = lax.axis_size("y")
    block_rows = local_rows * rows_y * cores // frame_blocks
    halves = local_rows // block_rows
    swap = [(0, 1), (1, 0)]

    def spread(packed):
        return lax.all_to_all(packed, ("x", "y"), split_axis=0, concat_axis=0, tiled=True)

    def onward(carried, distance):
        route = [(z, (z + distance) % depths) for z in range(depths)]
        route += [(depths + z, depths + (z - distance) % depths) for z in range(depths)]
        return lax.ppermute(carried, ("core", "z"), route)

    anchors = (frame_blocks - offsets % frame_blocks) % frame_blocks
    residue = lax.dynamic_index_in_dim(anchors, plane * depths + depth, keepdims=False) % 4
    packed = jnp.stack([jnp.transpose(keys, (1, 0, 2)), jnp.transpose(values, (1, 0, 2))], axis=1)
    block = lax.dynamic_slice_in_dim(packed, (residue % 2) * block_rows, block_rows, axis=2)
    block = jnp.where(residue // 2 == core, block, lax.ppermute(block, "core", swap))
    block = spread(block)

    slot_ids = jnp.arange(planes, dtype=jnp.int32)
    own_frames = slot_ids * depths + depth
    own_anchors = lax.dynamic_index_in_dim(
        anchors.reshape(planes, depths), depth, 1, keepdims=False
    )
    parts = jnp.arange(4, dtype=jnp.int32)
    parts = parts * 2 - 3 * (parts // 2)
    row_y = (own_anchors[:, None] // 4 + parts[None, :]) % 4
    index = (slot_ids[:, None] * rows_y + row_y).reshape(-1)
    held = jnp.take(block, index, axis=0).reshape(planes, 4, 2, block_rows, head_dim)

    head_queries = spread(after(jnp.transpose(queries, (1, 0, 2)), held))
    own_pair = spread(after(packed, head_queries))
    head_queries = head_queries.reshape(planes, rows_y * local_rows, head_dim)
    own_pair = own_pair.reshape(planes, rows_y, 2, local_rows, head_dim)
    partner_pair = lax.ppermute(own_pair, "core", swap)

    own_mask = lax.dynamic_index_in_dim(
        block_mask.reshape(planes, depths, frame_blocks, frame_blocks), depth, 1, keepdims=False
    )
    split_mask = own_mask.reshape(planes, rows_y, cores, halves, frame_blocks)
    query_mask = lax.dynamic_index_in_dim(split_mask, core, 2, keepdims=False)
    query_mask = query_mask.reshape(planes, -1, frame_blocks).astype(jnp.bfloat16)
    near_steps = lax.iota(jnp.int32, 6) % 3 + 1
    near_signs = (1 - 2 * (lax.iota(jnp.int32, 6) // 3)) * (2 * core - 1)
    shifts = (depth + near_signs * near_steps) // depths + planes

    calls, entries = [], []

    def begin():
        calls.append(([], [], [len(entries)]))

    def end():
        while len(entries) % 2:
            entries.append((3, 1, 0, 0, 0))
        calls[-1][2].append(len(entries))

    def anchor(which, entry, side, distance):
        calls[-1][1].append((which, "anchor", entry))
        entries.extend((2, side, distance, 0, place) for place in range(planes))

    def extra(which, entry, side, distance, part):
        shift = (0 if side == 1 else 3) + distance - 1
        calls[-1][1].append((which, "extra", (shift, entry)))
        entries.append((1, side, distance, part, 0))

    def own(which, partner):
        calls[-1][1].append((which, "own", None))
        spacing = frame_blocks // rows_y
        for y in range(rows_y):
            entries.extend((0, 1, 0, partner, spacing * y + j) for j in range(halves))

    def first_pieces(far, far_entry, near, near_entry, side):
        anchor(far, far_entry, side, 1)
        extra(near, near_entry, side, 1, 2)
        extra(near, near_entry + 1, side, 1, 1)
        extra(near, near_entry + 2, side, 1, 3)

    def second_pieces(far, far_entry, near, near_entry, side):
        anchor(far, far_entry, side, 2)
        anchor(far, far_entry + 1, side, 3)
        extra(near, near_entry, side, 2, 2)
        extra(near, near_entry + 1, side, 3, 2)

    begin()
    anchor(0, 0, 1, 0)
    first_pieces(1, 0, 2, 0, 1)
    end()
    begin()
    second_pieces(0, 0, 1, 0, 1)
    first_pieces(2, 0, 2, 1, -1)
    second_pieces(2, 4, 2, 6, -1)
    end()
    begin()
    own(0, 0)
    own(1, 1)
    for entry in range(3):
        anchor(2, entry, 1, 4 + entry)
    end()
    begin()
    for entry in range(2):
        anchor(0, entry, 1, 7 + entry)
    end()
    begin()
    for entry in range(4):
        anchor(0, entry, -1, 4 + entry)
    end()

    table = jnp.asarray(np.array(entries, np.int32).T)
    kind, side, distance, part, place = (table[row][None, :] for row in range(5))
    sign = (2 * core - 1) * side
    near = own_frames[:, None] + sign * distance
    far = place * depths + (depth + sign * distance + depths) % depths
    source = jnp.where(kind == 1, near, far)
    stride = jnp.where(distance == 1, strides[1], jnp.where(distance == 2, strides[2], strides[3]))
    fits = (near >= 0) & (near < frame_total) & ((4 * part) % stride == 0)
    valid = jnp.where(kind == 1, fits, source != own_frames[:, None])
    valid = (valid | (kind == 0)) & (kind != 3)
    every = jnp.arange(frame_total, dtype=jnp.int32)
    picked = jnp.where(source[:, :, None] == every, anchors, 0)
    column = (jnp.sum(picked, axis=2) + 4 * part) % frame_blocks
    column = jnp.where(kind == 0, place + halves * (core ^ part), column)
    code = jnp.repeat(jnp.where(valid, column, -1), block_rows, axis=1)
    chosen = jnp.arange(frame_blocks, dtype=jnp.int32)[None, :, None] == code[:, None, :]
    kept = jnp.einsum(
        "sbc,scn->sbn",
        query_mask,
        chosen.astype(jnp.bfloat16),
        preferred_element_type=jnp.float32,
    )
    bias = jnp.where(kept > 0.5, 0.0, masked_score)

    def run(number, arrays, state, last=False):
        pieces, (start, stop) = calls[number][1:]
        seen = bias[:, :, start * block_rows : stop * block_rows]
        return attend(
            head_queries, seen, shifts, arrays, pieces, state, last, block_rows
        )

    first = onward(held[:, :1], 1)
    near_first = onward(held[:, 1:], 1)
    second = onward(jnp.concatenate([held[:, :1], first], axis=1), 2)
    near_second = jnp.concatenate([held[:, 1:2], near_first[:, :1]], axis=1)
    near_second = onward(near_second, 2)
    third = onward(jnp.concatenate([first, second], axis=1), 3)
    fourth = onward(third[:, :2], 3)
    near = jnp.concatenate([first, near_first, second, near_second], axis=1)
    near_other = lax.ppermute(near, "core", swap)
    far_other = lax.ppermute(
        jnp.concatenate([third, fourth[:, :1]], axis=1), "core", swap
    )
    state = run(0, [held[:, :1], first, near_first], None)
    state = run(1, [second, near_second, near_other], state)
    state = run(2, [own_pair, partner_pair, third], state)
    state = run(3, [fourth], state)
    state = run(4, [far_other], state, last=True)

    output = state[0].reshape(planes * rows_y, local_rows, head_dim)
    return jnp.transpose(spread(output), (1, 0, 2))


def solution(mesh):
    grid = Mesh(mesh.devices.reshape(4, 2, 4, 16), ("y", "core", "x", "z"))
    tokens = P(("x", "z", "y", "core"), None, None)
    return jax.shard_map(
        local,
        mesh=grid,
        in_specs=(tokens, tokens, tokens, P(), P(), P()),
        out_specs=tokens,
        check_vma=False,
    )
```

time: 194 us -> 179 us (0.923)
  local copies, waits for them, and re-layouts: 30.8 us -> 12.6 us
  waiting for transfers between devices: 11.7 us -> 25.5 us
  starting transfers between devices: 76.7 us -> 66.5 us
  other arithmetic: 4.44 us -> 7.35 us
  between operations: 5.43 us -> 2.58 us
    gather x24 -> x1, local copies, waits for them, and re-layouts: 15.4 us -> 0.65 us  [local(): jnp.take(block, index, axis=0).reshape(planes, 4, 2, block_rows, head_dim)]
    ppermute x15 -> x9, starting transfers between devices: 58.9 us -> 50.2 us  [the longest x6 22.9 us: onward(): return lax.ppermute(carried, ('core', 'z'), route)]
    ppermute x15 -> x9, waiting for transfers between devices: 9.78 us -> 17.9 us  [the longest x6 17.9 us: onward(): return lax.ppermute(carried, ('core', 'z'), route)]
    all_to_all x2 -> x3, waiting for transfers between devices: 1.87 us -> 7.56 us  [spread(): lax.all_to_all(packed, ('x', 'y'), split_axis=0, concat_axis=0, tiled=True)]
    slice x4 -> x10, local copies, waits for them, and re-layouts: 1.35 us -> 4.86 us  [the longest x4 2.72 us: run(): seen = bias[:, :, start * block_rows:stop * block_rows]]
    ppermute x1, starting transfers between devices: 4.82 us -> 1.92 us  [local(): partner_pair = lax.ppermute(own_pair, 'core', swap)]
    reshape x4 -> x1, local copies, waits for them, and re-layouts: 2.94 us -> 0.08 us  [local(): anchors.reshape(planes, depths)]
    unnamed x37 -> x55, local copies, waits for them, and re-layouts: 4.03 us -> 2.34 us
  transfers between devices with their start and end apart: 18 -> 13, of which waited for: 4 -> 4; matrix products, arithmetic and copies ran while one was open for 15% -> 7% of each run, Pallas kernels for 18% -> 21%
where the time goes in v2:
time: 179 us; the launch traced here: 177 us
  starting transfers between devices  66.5 us (37%)
  Pallas kernels  45.3 us (25%)
  waiting for transfers between devices  25.5 us (14%)
  blocking collectives  17.1 us (10%)
  local copies, waits for them, and re-layouts  12.6 us (7%)
  other arithmetic  7.35 us (4%)
  between operations  2.58 us (1%)
    pallas_call x5, Pallas kernels, attend(): pl.pallas_call(functools.partial(attend_kernel, plan, state is None, last...  45.3 us
    ppermute x6, starting transfers between devices, onward(): return lax.ppermute(carried, ('core', 'z'), route)  22.9 us
    ppermute x6, waiting for transfers between devices, onward(): return lax.ppermute(carried, ('core', 'z'), route)  17.9 us
    all_to_all x1, blocking collectives, spread(): lax.all_to_all(packed, ('x', 'y'), split_axis=0, concat_axis=0, tiled=True)  17.1 us
    ppermute x1, starting transfers between devices, local(): lax.ppermute(jnp.concatenate([third, fourth[:, :1]], axis=1), 'core', swap)  15.3 us
    all_to_all x3, starting transfers between devices, spread(): lax.all_to_all(packed, ('x', 'y'), split_axis=0, concat_axis=0, tiled=True)  14.4 us
    ppermute x1, starting transfers between devices, local(): lax.ppermute(block, 'core', swap)  8.75 us
    all_to_all x3, waiting for transfers between devices, spread(): lax.all_to_all(packed, ('x', 'y'), split_axis=0, concat_axis=0, tiled=True)  7.56 us
  transfers between devices with their start and end apart: 13, of which 4 were waited for; matrix products, arithmetic and copies ran while one was open for 7% of the time, Pallas kernels for 21%

profile of v2, /device:TPU:1, one launch (start us, length us, event | category | flops | bytes accessed | tf_op | source)
XLA Modules:
  0.0 177.3 jit_solution(1027648844604587854)
XLA Ops:
  3.2 1.5 copy_bitcast_fusion
  4.8 8.7 %collective-permute-start = (bf16[16,2,64,128]{3,2,1,0:T(8,128)(2,1)S(1)}, bf16[16,2,64,128]{3,2,1,0:T(8,128)(2,1)S(1)}, u32[]{:S(2)}, u32[]{:S(2)}) collective-permute-start(bf16[16,2,64,128]{3,2,1,0:T(8,128)(2,1)S(1)} %fusion.2), channel_id=1, source_target_pairs={{0,64},{64,0},{1,65},{65,1},{2,66},{66,2},{3,67},{67,3},{4,68},{68... | collective-permute-start | bytes 1572872 | tf_op jit(solution)/shard_map/ppermute | solution.py:183
  13.6 1.1 pad_maximum_fusion
  16.0 1.0 broadcast_select_fusion
  17.1 3.7 %all-to-all-start = ((bf16[16,2,64,128]{3,2,1,0:T(8,128)(2,1)}), bf16[16,2,64,128]{3,2,1,0:T(8,128)(2,1)S(1)}, u32[]{:S(2)}, u32[]{:S(2)}) async-start(bf16[16,2,64,128]{3,2,1,0:T(8,128)(2,1)} %broadcast_select_fusion), calls=%async_computation | async-start | bytes 1048576 | tf_op jit(solution)/shard_map/all_to_all | solution.py:172
  20.9 0.9 copy.34
  21.8 2.0 %compare_bitcast_fusion = pred[92]{0:T(512)(128)(4,1)S(1)} fusion(s32[1,92]{1,0:T(1,128)S(1)} %copy-done.20, pred[1,92]{1,0:T(4,128)(4,1)S(1)} %copy-done.21, pred[1,92]{1,0:T(4,128)(4,1)S(1)} %copy-done.22, s32[]{:T(128)} %bitcast.14, s32[]{:T(128)} %bitcast.13, s32[]{:T(128)} %bitcast.12), kind=kLoop, calls=%fused_computation.62 | loop fusion | flops 1196 | bytes 656 | tf_op jit(solution)/shard_map/and | solution.py:281
  23.8 7.6 %all-to-all-done = bf16[16,2,64,128]{3,2,1,0:T(8,128)(2,1)S(1)} async-done(((bf16[16,2,64,128]{3,2,1,0:T(8,128)(2,1)}), bf16[16,2,64,128]{3,2,1,0:T(8,128)(2,1)S(1)}, u32[]{:S(2)}, u32[]{:S(2)}) %all-to-all-start) | async-done | bytes 524320 | tf_op jit(solution)/shard_map/all_to_all | solution.py:172
  32.2 4.0 %all-to-all-start.1 = ((bf16[16,128,128]{2,1,0:T(8,128)(2,1)}), bf16[16,128,128]{2,1,0:T(8,128)(2,1)S(1)}, u32[]{:S(2)}, u32[]{:S(2)}) async-start(bf16[16,128,128]{2,1,0:T(8,128)(2,1)} %bitcast.34), calls=%async_computation.1 | async-start | bytes 1048576 | tf_op jit(solution)/shard_map/all_to_all | solution.py:172
  36.6 0.8 slice.88
  37.4 8.8 %collective-permute-start.7 = (bf16[4,3,2,64,128]{4,3,2,1,0:T(8,128)(2,1)}, bf16[4,3,2,64,128]{4,3,2,1,0:T(8,128)(2,1)S(1)}, u32[]{:S(2)}, u32[]{:S(2)}) collective-permute-start(bf16[4,3,2,64,128]{4,3,2,1,0:T(8,128)(2,1)} %slice.88), channel_id=1, source_target_pairs={{0,1},{1,2},{2,3},{3,4},{4,5},{5,6},{6,7},{7,8},{8,9},{9,10},{10,1... | collective-permute-start | bytes 1179656 | tf_op jit(solution)/shard_map/ppermute | solution.py:177
  46.9 2.6 %collective-permute-start.1 = (bf16[4,1,2,64,128]{4,3,2,1,0:T(8,128)(2,1)S(1)}, bf16[4,1,2,64,128]{4,3,2,1,0:T(8,128)(2,1)S(1)}, u32[]{:S(2)}, u32[]{:S(2)}) collective-permute-start(bf16[4,1,2,64,128]{4,3,2,1,0:T(8,128)(2,1)S(1)} %get-tuple-element.28.refs_0_), channel_id=1, source_target_pairs={{0,1},{1,2},{2,3},{3,4},{4,5},{5,6},{6,7},{7,8},{8,9},{9,10},{10,1... | collective-permute-start | bytes 393224 | tf_op jit(solution)/shard_map/ppermute | solution.py:177
  50.3 6.7 %all-to-all-start.2 = ((bf16[16,2,128,128]{3,2,1,0:T(8,128)(2,1)}), bf16[16,2,128,128]{3,2,1,0:T(8,128)(2,1)S(1)}, u32[]{:S(2)}, u32[]{:S(2)}) async-start(bf16[16,2,128,128]{3,2,1,0:T(8,128)(2,1)} %pad_maximum_fusion), calls=%async_computation.2 | async-start | bytes 2097152 | tf_op jit(solution)/shard_map/all_to_all | solution.py:172
  58.0 3.1 %collective-permute-start.2 = (bf16[4,2,2,64,128]{4,3,2,1,0:T(8,128)(2,1)S(1)}, bf16[4,2,2,64,128]{4,3,2,1,0:T(8,128)(2,1)S(1)}, u32[]{:S(2)}, u32[]{:S(2)}) collective-permute-start(bf16[4,2,2,64,128]{4,3,2,1,0:T(8,128)(2,1)S(1)} %pad_maximum_fusion.4), channel_id=1, source_target_pairs={{0,2},{1,3},{2,4},{3,5},{4,6},{5,7},{6,8},{7,9},{8,10},{9,11},{10,... | collective-permute-start | bytes 786440 | tf_op jit(solution)/shard_map/ppermute | solution.py:177
  61.2 4.3 %collective-permute-start.8 = (bf16[4,2,2,64,128]{4,3,2,1,0:T(8,128)(2,1)S(1)}, bf16[4,2,2,64,128]{4,3,2,1,0:T(8,128)(2,1)S(1)}, u32[]{:S(2)}, u32[]{:S(2)}) collective-permute-start(bf16[4,2,2,64,128]{4,3,2,1,0:T(8,128)(2,1)S(1)} %pad_maximum_fusion.5), channel_id=1, source_target_pairs={{0,2},{1,3},{2,4},{3,5},{4,6},{5,7},{6,8},{7,9},{8,10},{9,11},{10,... | collective-permute-start | bytes 786440 | tf_op jit(solution)/shard_map/ppermute | solution.py:177
  65.6 6.3 %collective-permute-done.2.refs_0_ = bf16[4,2,2,64,128]{4,3,2,1,0:T(8,128)(2,1)S(1)} collective-permute-done((bf16[4,2,2,64,128]{4,3,2,1,0:T(8,128)(2,1)S(1)}, bf16[4,2,2,64,128]{4,3,2,1,0:T(8,128)(2,1)S(1)}, u32[]{:S(2)}, u32[]{:S(2)}) %collective-permute-start.2) | collective-permute-done | bytes 262176 | tf_op jit(solution)/shard_map/ppermute | solution.py:177
  72.0 0.9 pad_maximum_fusion.3
  72.8 1.9 %collective-permute-start.3 = (bf16[4,3,2,64,128]{4,3,2,1,0:T(8,128)(2,1)}, bf16[4,3,2,64,128]{4,3,2,1,0:T(8,128)(2,1)S(1)}, u32[]{:S(2)}, u32[]{:S(2)}) collective-permute-start(bf16[4,3,2,64,128]{4,3,2,1,0:T(8,128)(2,1)} %pad_maximum_fusion.3), channel_id=1, source_target_pairs={{0,3},{1,4},{2,5},{3,6},{4,7},{5,8},{6,9},{7,10},{8,11},{9,12},{10... | collective-permute-start | bytes 1179656 | tf_op jit(solution)/shard_map/ppermute | solution.py:177
  75.4 3.3 %collective-permute-start.9 = (bf16[4,8,2,64,128]{4,3,2,1,0:T(8,128)(2,1)S(1)}, bf16[4,8,2,64,128]{4,3,2,1,0:T(8,128)(2,1)}, u32[]{:S(2)}, u32[]{:S(2)}) collective-permute-start(bf16[4,8,2,64,128]{4,3,2,1,0:T(8,128)(2,1)S(1)} %pad_maximum_fusion.1), channel_id=1, source_target_pairs={{0,64},{64,0},{1,65},{65,1},{2,66},{66,2},{3,67},{67,3},{4,68},{68... | collective-permute-start | bytes 3145736 | tf_op jit(solution)/shard_map/ppermute | solution.py:313
  79.1 1.9 %collective-permute-start.6 = (bf16[4,4,2,128,128]{4,3,2,1,0:T(8,128)(2,1)S(1)}, bf16[4,4,2,128,128]{4,3,2,1,0:T(8,128)(2,1)}, u32[]{:S(2)}, u32[]{:S(2)}) collective-permute-start(bf16[4,4,2,128,128]{4,3,2,1,0:T(8,128)(2,1)S(1)} %bitcast.42), channel_id=1, source_target_pairs={{0,64},{64,0},{1,65},{65,1},{2,66},{66,2},{3,67},{67,3},{4,68},{68... | collective-permute-start | bytes 3145736 | tf_op jit(solution)/shard_map/ppermute | solution.py:201
  81.3 5.6 %collective-permute-done.3.refs_2_ = bf16[4,3,2,64,128]{4,3,2,1,0:T(8,128)(2,1)S(1)} collective-permute-done((bf16[4,3,2,64,128]{4,3,2,1,0:T(8,128)(2,1)}, bf16[4,3,2,64,128]{4,3,2,1,0:T(8,128)(2,1)S(1)}, u32[]{:S(2)}, u32[]{:S(2)}) %collective-permute-start.3) | collective-permute-done | bytes 393248 | tf_op jit(solution)/shard_map/ppermute | solution.py:177
  86.9 2.2 %collective-permute-start.4 = (bf16[4,2,2,64,128]{4,3,2,1,0:T(8,128)(2,1)S(1)}, bf16[4,2,2,64,128]{4,3,2,1,0:T(8,128)(2,1)S(1)}, u32[]{:S(2)}, u32[]{:S(2)}) collective-permute-start(bf16[4,2,2,64,128]{4,3,2,1,0:T(8,128)(2,1)S(1)} %slice.82), channel_id=1, source_target_pairs={{0,3},{1,4},{2,5},{3,6},{4,7},{5,8},{6,9},{7,10},{8,11},{9,12},{10... | collective-permute-start | bytes 786440 | tf_op jit(solution)/shard_map/ppermute | solution.py:177
  89.1 0.8 fusion.35
  89.9 6.0 %collective-permute-done.4.refs_0_ = bf16[4,2,2,64,128]{4,3,2,1,0:T(8,128)(2,1)S(1)} collective-permute-done((bf16[4,2,2,64,128]{4,3,2,1,0:T(8,128)(2,1)S(1)}, bf16[4,2,2,64,128]{4,3,2,1,0:T(8,128)(2,1)S(1)}, u32[]{:S(2)}, u32[]{:S(2)}) %collective-permute-start.4) | collective-permute-done | bytes 262176 | tf_op jit(solution)/shard_map/ppermute | solution.py:177
  96.0 15.3 %collective-permute-start.5 = (bf16[4,4,2,64,128]{4,3,2,1,0:T(8,128)(2,1)S(1)}, bf16[4,4,2,64,128]{4,3,2,1,0:T(8,128)(2,1)}, u32[]{:S(2)}, u32[]{:S(2)}) collective-permute-start(bf16[4,4,2,64,128]{4,3,2,1,0:T(8,128)(2,1)S(1)} %pad_maximum_fusion.2), channel_id=1, source_target_pairs={{0,64},{64,0},{1,65},{65,1},{2,66},{66,2},{3,67},{67,3},{4,68},{68... | collective-permute-start | bytes 1572872 | tf_op jit(solution)/shard_map/ppermute | solution.py:314
  113.8 6.7 %shard_map.73 = (f32[4,512,128]{2,1,0:T(8,128)}, f32[4,512,128]{2,1,0:T(8,128)}) custom-call(s32[6]{0:T(128)} %fusion.34.shifts, bf16[4,512,128]{2,1,0:T(8,128)(2,1)} %bitcast.35, f32[4,8,768]{2,1,0:T(8,128)} %slice.90.bias, bf16[4,1,2,64,128]{4,3,2,1,0:T(8,128)(2,1)} %copy-done.8, bf16[4,1,2,64,128]{4,3,2,1,0:T(8,128)(2,1)} %copy-done.1, ...), custom_call_target="tpu_custom_call" | custom-call | flops 805306368 | bytes 8388608 | tf_op jit(solution)/shard_map/pallas_call | solution.py:133
  120.5 11.6 %shard_map.74 = (f32[4,512,128]{2,1,0:T(8,128)}, f32[4,512,128]{2,1,0:T(8,128)}) custom-call(s32[6]{0:T(128)} %fusion.34.shifts, bf16[4,512,128]{2,1,0:T(8,128)(2,1)} %bitcast.36, f32[4,8,1792]{2,1,0:T(8,128)} %get-tuple-element.25.bias, bf16[4,2,2,64,128]{4,3,2,1,0:T(8,128)(2,1)} %copy-done.4, bf16[4,2,2,64,128]{4,3,2,1,0:T(8,128)(2,1)} %copy-done.10, ...), custom_call_target="tpu_custom_call" | custom-call | flops 1879048192 | bytes 8388608 | tf_op jit(solution)/shard_map/pallas_call | solution.py:133
  132.1 11.5 %shard_map.75 = (f32[4,512,128]{2,1,0:T(8,128)}, f32[4,512,128]{2,1,0:T(8,128)}) custom-call(s32[6]{0:T(128)} %fusion.34.shifts, bf16[4,512,128]{2,1,0:T(8,128)(2,1)} %bitcast.37, f32[4,8,1792]{2,1,0:T(8,128)} %get-tuple-element.26.bias, bf16[4,4,2,128,128]{4,3,2,1,0:T(8,128)(2,1)} %bitcast.43, bf16[4,4,2,128,128]{4,3,2,1,0:T(8,128)(2,1)} %collective-permute-done.6.refs_1_, ...), custom_call_target="tpu_custom_call" | custom-call | flops 1879048192 | bytes 8388608 | tf_op jit(solution)/shard_map/pallas_call | solution.py:133
  143.7 6.9 %shard_map.76 = (f32[4,512,128]{2,1,0:T(8,128)}, f32[4,512,128]{2,1,0:T(8,128)}) custom-call(s32[6]{0:T(128)} %fusion.34.shifts, bf16[4,512,128]{2,1,0:T(8,128)(2,1)} %bitcast.38, f32[4,8,512]{2,1,0:T(8,128)} %slice.84.bias, bf16[4,2,2,64,128]{4,3,2,1,0:T(8,128)(2,1)} %copy-done.6, f32[4,512,128]{2,1,0:T(8,128)} %get-tuple-element.21.refs_1_, ...), custom_call_target="tpu_custom_call" | custom-call | flops 536870912 | bytes 8388608 | tf_op jit(solution)/shard_map/pallas_call | solution.py:133
  150.6 8.5 %shard_map.77 = bf16[4,512,128]{2,1,0:T(8,128)(2,1)} custom-call(s32[6]{0:T(128)} %fusion.34.shifts, bf16[4,512,128]{2,1,0:T(8,128)(2,1)} %bitcast.39, f32[4,8,1024]{2,1,0:T(8,128)} %slice.80.bias, bf16[4,4,2,64,128]{4,3,2,1,0:T(8,128)(2,1)} %collective-permute-done.5.refs_0_, f32[4,512,128]{2,1,0:T(8,128)} %get-tuple-element.23.refs_1_, ...), custom_call_target="tpu_custom_call" | custom-call | flops 1073741824 | bytes 8388608 | tf_op jit(solution)/shard_map/pallas_call | solution.py:133
  159.1 17.1 %all_to_all.20 = bf16[16,128,128]{2,1,0:T(8,128)(2,1)S(1)} all-to-all(bf16[16,128,128]{2,1,0:T(8,128)(2,1)} %bitcast.44), channel_id=1, replica_groups=mesh['y'=4,'core'=2,'x'=4,'z'=16] {'x','y'}, dimensions={0} | all-to-all | bytes 1048576 | tf_op jit(solution)/shard_map/all_to_all | solution.py:172
  176.2 1.1 copy.30
  (104 shorter events, 10.2 us)
Async XLA Ops:
  4.8 11.3 %collective-permute-start = (bf16[16,2,64,128]{3,2,1,0:T(8,128)(2,1)S(1)}, bf16[16,2,64,128]{3,2,1,0:T(8,128)(2,1)S(1)}, u32[]{:S(2)}, u32[]{:S(2)}) collective-permute-start(bf16[16,2,64,128]{3,2,1,0:T(8,128)(2,1)S(1)} %fusion.2), channel_id=1, source_target_pairs={{0,64},{64,0},{1,65},{65,1},{2,66},{66,2},{3,67},{67,3},{4,68},{68... | collective-permute-start | bytes 1572872 | tf_op jit(solution)/shard_map/ppermute | solution.py:183
  17.1 4.7 %copy-start.23 = (s32[1,92]{1,0:T(1,128)S(1)}, s32[1,92]{1,0:T(1,128)}, u32[]{:S(2)}) copy-start(s32[1,92]{1,0:T(1,128)} %constant.218) | copy-start | bytes 1108
  17.1 4.7 %copy-start.24 = (s32[1,92]{1,0:T(1,128)S(1)}, s32[1,92]{1,0:T(1,128)}, u32[]{:S(2)}) copy-start(s32[1,92]{1,0:T(1,128)} %constant.224) | copy-start | bytes 1108
  17.1 4.7 %copy-start.20 = (s32[1,92]{1,0:T(1,128)S(1)}, s32[1,92]{1,0:T(1,128)}, u32[]{:S(2)}) copy-start(s32[1,92]{1,0:T(1,128)} %constant.214) | copy-start | bytes 1108
  17.1 4.7 %copy-start.21 = (pred[1,92]{1,0:T(4,128)(4,1)S(1)}, pred[1,92]{1,0:T(4,128)(4,1)}, u32[]{:S(2)}) copy-start(pred[1,92]{1,0:T(4,128)(4,1)} %constant.215) | copy-start | bytes 280
  17.1 4.7 %copy-start.22 = (pred[1,92]{1,0:T(4,128)(4,1)S(1)}, pred[1,92]{1,0:T(4,128)(4,1)}, u32[]{:S(2)}) copy-start(pred[1,92]{1,0:T(4,128)(4,1)} %constant.216) | copy-start | bytes 280
  17.1 14.3 %all-to-all-start = ((bf16[16,2,64,128]{3,2,1,0:T(8,128)(2,1)}), bf16[16,2,64,128]{3,2,1,0:T(8,128)(2,1)S(1)}, u32[]{:S(2)}, u32[]{:S(2)}) async-start(bf16[16,2,64,128]{3,2,1,0:T(8,128)(2,1)} %broadcast_select_fusion), calls=%async_computation | async-start | bytes 1048576 | tf_op jit(solution)/shard_map/all_to_all | solution.py:172
  32.1 4.2 %copy-start.11 = (s32[64,16,16]{0,2,1:T(8,128)S(1)}, s32[64,16,16]{0,2,1:T(8,128)}, u32[]{:S(2)}) copy-start(s32[64,16,16]{0,2,1:T(8,128)} %param.10) | copy-start | bytes 196612
  32.2 4.4 %copy-start.13 = (pred[92]{0:T(512)(128)(4,1)S(1)}, pred[92]{0:T(512)(128)(4,1)}, u32[]{:S(2)}) copy-start(pred[92]{0:T(512)(128)(4,1)} %constant.210) | copy-start | bytes 280
  32.2 17.3 %all-to-all-start.1 = ((bf16[16,128,128]{2,1,0:T(8,128)(2,1)}), bf16[16,128,128]{2,1,0:T(8,128)(2,1)S(1)}, u32[]{:S(2)}, u32[]{:S(2)}) async-start(bf16[16,128,128]{2,1,0:T(8,128)(2,1)} %bitcast.34), calls=%async_computation.1 | async-start | bytes 1048576 | tf_op jit(solution)/shard_map/all_to_all | solution.py:172
  36.3 13.3 %copy-start.15 = (s32[4]{0:T(128)}, s32[4]{0:T(128)S(1)}, u32[]{:S(2)}) copy-start(s32[4]{0:T(128)S(1)} %multiply_add_fusion.1) | copy-start | bytes 52
  37.4 23.7 %collective-permute-start.7 = (bf16[4,3,2,64,128]{4,3,2,1,0:T(8,128)(2,1)}, bf16[4,3,2,64,128]{4,3,2,1,0:T(8,128)(2,1)S(1)}, u32[]{:S(2)}, u32[]{:S(2)}) collective-permute-start(bf16[4,3,2,64,128]{4,3,2,1,0:T(8,128)(2,1)} %slice.88), channel_id=1, source_target_pairs={{0,1},{1,2},{2,3},{3,4},{4,5},{5,6},{6,7},{7,8},{8,9},{9,10},{10,1... | collective-permute-start | bytes 1179656 | tf_op jit(solution)/shard_map/ppermute | solution.py:177
  46.9 11.1 %copy-start.8 = (bf16[4,1,2,64,128]{4,3,2,1,0:T(8,128)(2,1)}, bf16[4,1,2,64,128]{4,3,2,1,0:T(8,128)(2,1)S(1)}, u32[]{:S(2)}) copy-start(bf16[4,1,2,64,128]{4,3,2,1,0:T(8,128)(2,1)S(1)} %get-tuple-element.28.refs_0_) | copy-start | bytes 393220
  46.9 11.1 %collective-permute-start.1 = (bf16[4,1,2,64,128]{4,3,2,1,0:T(8,128)(2,1)S(1)}, bf16[4,1,2,64,128]{4,3,2,1,0:T(8,128)(2,1)S(1)}, u32[]{:S(2)}, u32[]{:S(2)}) collective-permute-start(bf16[4,1,2,64,128]{4,3,2,1,0:T(8,128)(2,1)S(1)} %get-tuple-element.28.refs_0_), channel_id=1, source_target_pairs={{0,1},{1,2},{2,3},{3,4},{4,5},{5,6},{6,7},{7,8},{8,9},{9,10},{10,1... | collective-permute-start | bytes 393224 | tf_op jit(solution)/shard_map/ppermute | solution.py:177
  50.3 28.7 %all-to-all-start.2 = ((bf16[16,2,128,128]{3,2,1,0:T(8,128)(2,1)}), bf16[16,2,128,128]{3,2,1,0:T(8,128)(2,1)S(1)}, u32[]{:S(2)}, u32[]{:S(2)}) async-start(bf16[16,2,128,128]{3,2,1,0:T(8,128)(2,1)} %pad_maximum_fusion), calls=%async_computation.2 | async-start | bytes 2097152 | tf_op jit(solution)/shard_map/all_to_all | solution.py:172
  57.3 8.2 %copy-start.14 = (pred[92]{0:T(512)(128)(4,1)S(1)}, pred[92]{0:T(512)(128)(4,1)}, u32[]{:S(2)}) copy-start(pred[92]{0:T(512)(128)(4,1)} %constant.210) | copy-start | bytes 280
  57.4 8.2 %copy-start.16 = (s32[4]{0:T(128)S(1)}, s32[4]{0:T(128)}, u32[]{:S(2)}) copy-start(s32[4]{0:T(128)} %copy-done.15) | copy-start | bytes 52
  57.4 8.2 %copy-start.17 = (pred[92]{0:T(512)(128)(4,1)S(1)}, pred[92]{0:T(512)(128)(4,1)}, u32[]{:S(2)}) copy-start(pred[92]{0:T(512)(128)(4,1)} %constant.220) | copy-start | bytes 280
  57.4 8.2 %copy-start.18 = (pred[92]{0:T(512)(128)(4,1)S(1)}, pred[92]{0:T(512)(128)(4,1)}, u32[]{:S(2)}) copy-start(pred[92]{0:T(512)(128)(4,1)} %constant.222) | copy-start | bytes 280
  57.4 8.2 %copy-start.19 = (s32[92]{0:T(128)S(1)}, s32[92]{0:T(128)}, u32[]{:S(2)}) copy-start(s32[92]{0:T(128)} %constant.223) | copy-start | bytes 1108
  58.0 16.8 %copy-start.1 = (bf16[4,1,2,64,128]{4,3,2,1,0:T(8,128)(2,1)}, bf16[4,1,2,64,128]{4,3,2,1,0:T(8,128)(2,1)S(1)}, u32[]{:S(2)}) copy-start(bf16[4,1,2,64,128]{4,3,2,1,0:T(8,128)(2,1)S(1)} %collective-permute-done.1.refs_1_) | copy-start | bytes 393220
  58.0 13.9 %collective-permute-start.2 = (bf16[4,2,2,64,128]{4,3,2,1,0:T(8,128)(2,1)S(1)}, bf16[4,2,2,64,128]{4,3,2,1,0:T(8,128)(2,1)S(1)}, u32[]{:S(2)}, u32[]{:S(2)}) collective-permute-start(bf16[4,2,2,64,128]{4,3,2,1,0:T(8,128)(2,1)S(1)} %pad_maximum_fusion.4), channel_id=1, source_target_pairs={{0,2},{1,3},{2,4},{3,5},{4,6},{5,7},{6,8},{7,9},{8,10},{9,11},{10,... | collective-permute-start | bytes 786440 | tf_op jit(solution)/shard_map/ppermute | solution.py:177
  61.1 13.8 %copy-start.5 = (bf16[4,3,2,64,128]{4,3,2,1,0:T(8,128)(2,1)}, bf16[4,3,2,64,128]{4,3,2,1,0:T(8,128)(2,1)S(1)}, u32[]{:S(2)}) copy-start(bf16[4,3,2,64,128]{4,3,2,1,0:T(8,128)(2,1)S(1)} %collective-permute-done.7.refs_2_) | copy-start | bytes 1179652
  61.2 13.5 %collective-permute-start.8 = (bf16[4,2,2,64,128]{4,3,2,1,0:T(8,128)(2,1)S(1)}, bf16[4,2,2,64,128]{4,3,2,1,0:T(8,128)(2,1)S(1)}, u32[]{:S(2)}, u32[]{:S(2)}) collective-permute-start(bf16[4,2,2,64,128]{4,3,2,1,0:T(8,128)(2,1)S(1)} %pad_maximum_fusion.5), channel_id=1, source_target_pairs={{0,2},{1,3},{2,4},{3,5},{4,6},{5,7},{6,8},{7,9},{8,10},{9,11},{10,... | collective-permute-start | bytes 786440 | tf_op jit(solution)/shard_map/ppermute | solution.py:177
  72.8 14.1 %collective-permute-start.3 = (bf16[4,3,2,64,128]{4,3,2,1,0:T(8,128)(2,1)}, bf16[4,3,2,64,128]{4,3,2,1,0:T(8,128)(2,1)S(1)}, u32[]{:S(2)}, u32[]{:S(2)}) collective-permute-start(bf16[4,3,2,64,128]{4,3,2,1,0:T(8,128)(2,1)} %pad_maximum_fusion.3), channel_id=1, source_target_pairs={{0,3},{1,4},{2,5},{3,6},{4,7},{5,8},{6,9},{7,10},{8,11},{9,12},{10... | collective-permute-start | bytes 1179656 | tf_op jit(solution)/shard_map/ppermute | solution.py:177
  75.4 45.1 %collective-permute-start.9 = (bf16[4,8,2,64,128]{4,3,2,1,0:T(8,128)(2,1)S(1)}, bf16[4,8,2,64,128]{4,3,2,1,0:T(8,128)(2,1)}, u32[]{:S(2)}, u32[]{:S(2)}) collective-permute-start(bf16[4,8,2,64,128]{4,3,2,1,0:T(8,128)(2,1)S(1)} %pad_maximum_fusion.1), channel_id=1, source_target_pairs={{0,64},{64,0},{1,65},{65,1},{2,66},{66,2},{3,67},{67,3},{4,68},{68... | collective-permute-start | bytes 3145736 | tf_op jit(solution)/shard_map/ppermute | solution.py:313
  79.1 10.9 %copy-start.3 = (bf16[16,2,128,128]{3,2,1,0:T(8,128)(2,1)}, bf16[16,2,128,128]{3,2,1,0:T(8,128)(2,1)S(1)}, u32[]{:S(2)}) copy-start(bf16[16,2,128,128]{3,2,1,0:T(8,128)(2,1)S(1)} %all-to-all-done.2) | copy-start | bytes 3145732
  79.1 53.1 %collective-permute-start.6 = (bf16[4,4,2,128,128]{4,3,2,1,0:T(8,128)(2,1)S(1)}, bf16[4,4,2,128,128]{4,3,2,1,0:T(8,128)(2,1)}, u32[]{:S(2)}, u32[]{:S(2)}) collective-permute-start(bf16[4,4,2,128,128]{4,3,2,1,0:T(8,128)(2,1)S(1)} %bitcast.42), channel_id=1, source_target_pairs={{0,64},{64,0},{1,65},{65,1},{2,66},{66,2},{3,67},{67,3},{4,68},{68... | collective-permute-start | bytes 3145736 | tf_op jit(solution)/shard_map/ppermute | solution.py:201
  86.9 9.1 %copy-start.2 = (bf16[4,3,2,64,128]{4,3,2,1,0:T(8,128)(2,1)}, bf16[4,3,2,64,128]{4,3,2,1,0:T(8,128)(2,1)S(1)}, u32[]{:S(2)}) copy-start(bf16[4,3,2,64,128]{4,3,2,1,0:T(8,128)(2,1)S(1)} %collective-permute-done.3.refs_2_) | copy-start | bytes 1179652
  86.9 9.0 %collective-permute-start.4 = (bf16[4,2,2,64,128]{4,3,2,1,0:T(8,128)(2,1)S(1)}, bf16[4,2,2,64,128]{4,3,2,1,0:T(8,128)(2,1)S(1)}, u32[]{:S(2)}, u32[]{:S(2)}) collective-permute-start(bf16[4,2,2,64,128]{4,3,2,1,0:T(8,128)(2,1)S(1)} %slice.82), channel_id=1, source_target_pairs={{0,3},{1,4},{2,5},{3,6},{4,7},{5,8},{6,9},{7,10},{8,11},{9,12},{10... | collective-permute-start | bytes 786440 | tf_op jit(solution)/shard_map/ppermute | solution.py:177
  95.9 24.6 %copy-start.6 = (bf16[4,2,2,64,128]{4,3,2,1,0:T(8,128)(2,1)}, bf16[4,2,2,64,128]{4,3,2,1,0:T(8,128)(2,1)S(1)}, u32[]{:S(2)}) copy-start(bf16[4,2,2,64,128]{4,3,2,1,0:T(8,128)(2,1)S(1)} %collective-permute-done.4.refs_0_) | copy-start | bytes 786436
  96.0 54.6 %collective-permute-start.5 = (bf16[4,4,2,64,128]{4,3,2,1,0:T(8,128)(2,1)S(1)}, bf16[4,4,2,64,128]{4,3,2,1,0:T(8,128)(2,1)}, u32[]{:S(2)}, u32[]{:S(2)}) collective-permute-start(bf16[4,4,2,64,128]{4,3,2,1,0:T(8,128)(2,1)S(1)} %pad_maximum_fusion.2), channel_id=1, source_target_pairs={{0,64},{64,0},{1,65},{65,1},{2,66},{66,2},{3,67},{67,3},{4,68},{68... | collective-permute-start | bytes 1572872 | tf_op jit(solution)/shard_map/ppermute | solution.py:314
  (8 other events, 18.7 us)

commit v3 on v2

--- a/solution.py
+++ b/solution.py
@@ -64,6 +64,7 @@
     key_count, head_dim = key_buffer.shape
     factor = head_dim ** (-0.5) * log2_e
     groups = row_tile // block_rows
+    base = plan["base"]
     chunks = [(at, min(256, key_count - at)) for at in range(0, key_count, 256)]
 
     for tile in range(queries.shape[1] // row_tile):
@@ -77,7 +78,7 @@
                 (((1,), (1,)), ((), ())),
                 preferred_element_type=jnp.float32,
             )
-            seen = bias[0, tile * groups : (tile + 1) * groups, at : at + width]
+            seen = bias[0, tile * groups : (tile + 1) * groups, base + at : base + at + width]
             scores = scores.reshape(groups, block_rows, width) + seen[:, None, :]
             scores = scores.reshape(row_tile, width)
             score_buffer[:, at : at + width] = scores
@@ -111,9 +112,9 @@
             outs[1][0, rows] = summed
 
 
-def attend(queries, bias, shifts, arrays, pieces, state, last, block_rows):
+def attend(queries, bias, span, shifts, arrays, pieces, state, last, block_rows):
     slots, slot_rows, head_dim = queries.shape
-    key_count = bias.shape[-1]
+    key_count = span[1] - span[0]
     slot_spec = pl.BlockSpec((1, slot_rows, head_dim), lambda s, *_: (s, 0, 0))
     specs = [slot_spec, pl.BlockSpec((1,) + bias.shape[1:], lambda s, *_: (s, 0, 0))]
     for which, array in enumerate(arrays):
@@ -129,7 +130,7 @@
         out_shape = [state_shape] * 2
     carried = [] if state is None else list(state)
     specs += [slot_spec] * len(carried)
-    plan = {"arrays": len(arrays), "pieces": pieces}
+    plan = {"arrays": len(arrays), "pieces": pieces, "base": span[0]}
     return pl.pallas_call(
         functools.partial(attend_kernel, plan, state is None, last, block_rows),
         out_shape=out_shape,
@@ -235,26 +236,26 @@
         for y in range(rows_y):
             entries.extend((0, 1, 0, partner, spacing * y + j) for j in range(halves))
 
-    def first_pieces(far, far_entry, near, near_entry, side):
-        anchor(far, far_entry, side, 1)
-        extra(near, near_entry, side, 1, 2)
-        extra(near, near_entry + 1, side, 1, 1)
-        extra(near, near_entry + 2, side, 1, 3)
-
-    def second_pieces(far, far_entry, near, near_entry, side):
-        anchor(far, far_entry, side, 2)
-        anchor(far, far_entry + 1, side, 3)
-        extra(near, near_entry, side, 2, 2)
-        extra(near, near_entry + 1, side, 3, 2)
+    def first_pieces(which, entry, side):
+        anchor(which, entry, side, 1)
+        extra(which, entry + 1, side, 1, 2)
+        extra(which, entry + 2, side, 1, 1)
+        extra(which, entry + 3, side, 1, 3)
+
+    def second_pieces(which, entry, side):
+        anchor(which, entry, side, 2)
+        anchor(which, entry + 2, side, 3)
+        extra(which, entry + 1, side, 2, 2)
+        extra(which, entry + 3, side, 3, 2)
 
     begin()
     anchor(0, 0, 1, 0)
-    first_pieces(1, 0, 2, 0, 1)
-    end()
-    begin()
-    second_pieces(0, 0, 1, 0, 1)
-    first_pieces(2, 0, 2, 1, -1)
-    second_pieces(2, 4, 2, 6, -1)
+    first_pieces(1, 0, 1)
+    end()
+    begin()
+    second_pieces(0, 0, 1)
+    first_pieces(1, 0, -1)
+    second_pieces(1, 4, -1)
     end()
     begin()
     own(0, 0)
@@ -297,25 +298,23 @@
 
     def run(number, arrays, state, last=False):
         pieces, (start, stop) = calls[number][1:]
-        seen = bias[:, :, start * block_rows : stop * block_rows]
+        span = (start * block_rows, stop * block_rows)
         return attend(
-            head_queries, seen, shifts, arrays, pieces, state, last, block_rows
+            head_queries, bias, span, shifts, arrays, pieces, state, last, block_rows
         )
 
-    first = onward(held[:, :1], 1)
-    near_first = onward(held[:, 1:], 1)
-    second = onward(jnp.concatenate([held[:, :1], first], axis=1), 2)
-    near_second = jnp.concatenate([held[:, 1:2], near_first[:, :1]], axis=1)
-    near_second = onward(near_second, 2)
-    third = onward(jnp.concatenate([first, second], axis=1), 3)
+    first = onward(held, 1)
+    second = onward(jnp.concatenate([held[:, :2], first[:, :2]], axis=1), 2)
+    third = onward(
+        jnp.concatenate([first[:, :1], second[:, :1], second[:, 2:3]], axis=1), 3
+    )
     fourth = onward(third[:, :2], 3)
-    near = jnp.concatenate([first, near_first, second, near_second], axis=1)
-    near_other = lax.ppermute(near, "core", swap)
+    near_other = lax.ppermute(jnp.concatenate([first, second], axis=1), "core", swap)
     far_other = lax.ppermute(
         jnp.concatenate([third, fourth[:, :1]], axis=1), "core", swap
     )
-    state = run(0, [held[:, :1], first, near_first], None)
-    state = run(1, [second, near_second, near_other], state)
+    state = run(0, [held[:, :1], first], None)
+    state = run(1, [second, near_other], state)
     state = run(2, [own_pair, partner_pair, third], state)
     state = run(3, [fourth], state)
     state = run(4, [far_other], state, last=True)

time: 179 us -> 172 us (0.961)
  starting transfers between devices: 66.5 us -> 57.2 us
  waiting for transfers between devices: 25.5 us -> 29.4 us
  local copies, waits for them, and re-layouts: 12.6 us -> 9.46 us
    ppermute x1, starting transfers between devices: 15.3 us -> 9.68 us  [local(): lax.ppermute(jnp.concatenate([third, fourth[:, :1]], axis=1), 'core', swap)]
    all_to_all x3, waiting for transfers between devices: 7.56 us -> 12.6 us  [spread(): lax.all_to_all(packed, ('x', 'y'), split_axis=0, concat_axis=0, tiled=True)]
    ppermute x6 -> x4, starting transfers between devices: 22.9 us -> 18.2 us  [onward(): return lax.ppermute(carried, ('core', 'z'), route)]
    ppermute x1, starting transfers between devices: 3.32 us -> 7.04 us  [local(): lax.ppermute(jnp.concatenate([first, second], axis=1), 'core', swap)]
    slice x7 -> x5, local copies, waits for them, and re-layouts: 4.17 us -> 0.72 us  [the longest x1 0.65 us: local(): state = run(0, [held[:, :1], first], None)]
    all_to_all x3, starting transfers between devices: 14.4 us -> 11.6 us  [spread(): lax.all_to_all(packed, ('x', 'y'), split_axis=0, concat_axis=0, tiled=True)]
    ppermute x6 -> x4, waiting for transfers between devices: 17.9 us -> 15.9 us  [onward(): return lax.ppermute(carried, ('core', 'z'), route)]
  transfers between devices with their start and end apart: 13 -> 11, of which waited for: 4 -> 6; matrix products, arithmetic and copies ran while one was open for 7% -> 6% of each run, Pallas kernels for 21% -> 22%
where the time goes in v3:
time: 172 us; the launch traced here: 171 us
  starting transfers between devices  57.2 us (33%)
  Pallas kernels  45.8 us (27%)
  waiting for transfers between devices  29.4 us (17%)
  blocking collectives  17.7 us (10%)
  local copies, waits for them, and re-layouts  9.46 us (6%)
  other arithmetic  7.49 us (4%)
  between operations  2.5 us (1%)
    pallas_call x5, Pallas kernels, attend(): pl.pallas_call(functools.partial(attend_kernel, plan, state is None, last...  45.8 us
    ppermute x4, starting transfers between devices, onward(): return lax.ppermute(carried, ('core', 'z'), route)  18.2 us
    all_to_all x1, blocking collectives, spread(): lax.all_to_all(packed, ('x', 'y'), split_axis=0, concat_axis=0, tiled=True)  17.7 us
    ppermute x4, waiting for transfers between devices, onward(): return lax.ppermute(carried, ('core', 'z'), route)  15.9 us
    all_to_all x3, waiting for transfers between devices, spread(): lax.all_to_all(packed, ('x', 'y'), split_axis=0, concat_axis=0, tiled=True)  12.6 us
    all_to_all x3, starting transfers between devices, spread(): lax.all_to_all(packed, ('x', 'y'), split_axis=0, concat_axis=0, tiled=True)  11.6 us
    ppermute x1, starting transfers between devices, local(): lax.ppermute(jnp.concatenate([third, fourth[:, :1]], axis=1), 'core', swap)  9.68 us
    ppermute x1, starting transfers between devices, local(): lax.ppermute(block, 'core', swap)  8.75 us
  transfers between devices with their start and end apart: 11, of which 6 were waited for; matrix products, arithmetic and copies ran while one was open for 6% of the time, Pallas kernels for 22%

profile of v3, /device:TPU:1, one launch (start us, length us, event | category | flops | bytes accessed | tf_op | source)
XLA Modules:
  0.0 170.9 jit_solution(3298154126037888783)
XLA Ops:
  3.2 1.5 copy_bitcast_fusion
  4.8 8.7 %collective-permute-start = (bf16[16,2,64,128]{3,2,1,0:T(8,128)(2,1)S(1)}, bf16[16,2,64,128]{3,2,1,0:T(8,128)(2,1)S(1)}, u32[]{:S(2)}, u32[]{:S(2)}) collective-permute-start(bf16[16,2,64,128]{3,2,1,0:T(8,128)(2,1)S(1)} %fusion.2), channel_id=1, source_target_pairs={{0,64},{64,0},{1,65},{65,1},{2,66},{66,2},{3,67},{67,3},{4,68},{68... | collective-permute-start | bytes 1572872 | tf_op jit(solution)/shard_map/ppermute | solution.py:184
  14.1 0.9 collective-permute-done
  15.0 1.0 broadcast_select_fusion
  16.1 3.6 %all-to-all-start = ((bf16[16,2,64,128]{3,2,1,0:T(8,128)(2,1)}), bf16[16,2,64,128]{3,2,1,0:T(8,128)(2,1)S(1)}, u32[]{:S(2)}, u32[]{:S(2)}) async-start(bf16[16,2,64,128]{3,2,1,0:T(8,128)(2,1)} %broadcast_select_fusion), calls=%async_computation | async-start | bytes 1048576 | tf_op jit(solution)/shard_map/all_to_all | solution.py:173
  19.8 10.0 %all-to-all-done = bf16[16,2,64,128]{3,2,1,0:T(8,128)(2,1)S(1)} async-done(((bf16[16,2,64,128]{3,2,1,0:T(8,128)(2,1)}), bf16[16,2,64,128]{3,2,1,0:T(8,128)(2,1)S(1)}, u32[]{:S(2)}, u32[]{:S(2)}) %all-to-all-start) | async-done | bytes 524320 | tf_op jit(solution)/shard_map/all_to_all | solution.py:173
  30.6 9.2 %collective-permute-start.1 = (bf16[4,4,2,64,128]{4,3,2,1,0:T(8,128)(2,1)S(1)}, bf16[4,4,2,64,128]{4,3,2,1,0:T(8,128)(2,1)S(1)}, u32[]{:S(2)}, u32[]{:S(2)}) collective-permute-start(bf16[4,4,2,64,128]{4,3,2,1,0:T(8,128)(2,1)S(1)} %broadcast_select_fusion.1), channel_id=1, source_target_pairs={{0,1},{1,2},{2,3},{3,4},{4,5},{5,6},{6,7},{7,8},{8,9},{9,10},{10,1... | collective-permute-start | bytes 1572872 | tf_op jit(solution)/shard_map/ppermute | solution.py:178
  39.8 0.9 copy.34
  41.4 3.7 %all-to-all-start.1 = ((bf16[16,128,128]{2,1,0:T(8,128)(2,1)}), bf16[16,128,128]{2,1,0:T(8,128)(2,1)S(1)}, u32[]{:S(2)}, u32[]{:S(2)}) async-start(bf16[16,128,128]{2,1,0:T(8,128)(2,1)} %bitcast.34), calls=%async_computation.1 | async-start | bytes 1048576 | tf_op jit(solution)/shard_map/all_to_all | solution.py:173
  45.2 2.0 %compare_bitcast_fusion = pred[92]{0:T(512)(128)(4,1)S(1)} fusion(s32[1,92]{1,0:T(1,128)S(1)} %copy-done.13, pred[1,92]{1,0:T(4,128)(4,1)S(1)} %copy-done.14, pred[1,92]{1,0:T(4,128)(4,1)S(1)} %copy-done.15, s32[]{:T(128)} %bitcast.14, s32[]{:T(128)} %bitcast.13, s32[]{:T(128)} %bitcast.12), kind=kLoop, calls=%fused_computation.61 | loop fusion | flops 1196 | bytes 656 | tf_op jit(solution)/shard_map/and | solution.py:282
  47.2 1.1 pad_maximum_fusion
  48.4 3.1 %collective-permute-start.2 = (bf16[4,4,2,64,128]{4,3,2,1,0:T(8,128)(2,1)S(1)}, bf16[4,4,2,64,128]{4,3,2,1,0:T(8,128)(2,1)S(1)}, u32[]{:S(2)}, u32[]{:S(2)}) collective-permute-start(bf16[4,4,2,64,128]{4,3,2,1,0:T(8,128)(2,1)S(1)} %pad_maximum_fusion.2), channel_id=1, source_target_pairs={{0,2},{1,3},{2,4},{3,5},{4,6},{5,7},{6,8},{7,9},{8,10},{9,11},{10,... | collective-permute-start | bytes 1572872 | tf_op jit(solution)/shard_map/ppermute | solution.py:178
  51.5 2.6 %all-to-all-done.1 = bf16[16,128,128]{2,1,0:T(8,128)(2,1)S(1)} async-done(((bf16[16,128,128]{2,1,0:T(8,128)(2,1)}), bf16[16,128,128]{2,1,0:T(8,128)(2,1)S(1)}, u32[]{:S(2)}, u32[]{:S(2)}) %all-to-all-start.1) | async-done | bytes 524320 | tf_op jit(solution)/shard_map/all_to_all | solution.py:173
  54.9 4.3 %all-to-all-start.2 = ((bf16[16,2,128,128]{3,2,1,0:T(8,128)(2,1)}), bf16[16,2,128,128]{3,2,1,0:T(8,128)(2,1)}, u32[]{:S(2)}, u32[]{:S(2)}) async-start(bf16[16,2,128,128]{3,2,1,0:T(8,128)(2,1)} %pad_maximum_fusion), calls=%async_computation.2 | async-start | bytes 2097152 | tf_op jit(solution)/shard_map/all_to_all | solution.py:173
  59.6 3.4 %collective-permute-done.2.refs_0_ = bf16[4,4,2,64,128]{4,3,2,1,0:T(8,128)(2,1)S(1)} collective-permute-done((bf16[4,4,2,64,128]{4,3,2,1,0:T(8,128)(2,1)S(1)}, bf16[4,4,2,64,128]{4,3,2,1,0:T(8,128)(2,1)S(1)}, u32[]{:S(2)}, u32[]{:S(2)}) %collective-permute-start.2) | collective-permute-done | bytes 524320 | tf_op jit(solution)/shard_map/ppermute | solution.py:178
  63.1 1.2 pad_maximum_fusion.1
  64.3 7.0 %collective-permute-start.7 = (bf16[4,8,2,64,128]{4,3,2,1,0:T(8,128)(2,1)}, bf16[4,8,2,64,128]{4,3,2,1,0:T(8,128)(2,1)}, u32[]{:S(2)}, u32[]{:S(2)}) collective-permute-start(bf16[4,8,2,64,128]{4,3,2,1,0:T(8,128)(2,1)} %pad_maximum_fusion.1), channel_id=1, source_target_pairs={{0,64},{64,0},{1,65},{65,1},{2,66},{66,2},{3,67},{67,3},{4,68},{68... | collective-permute-start | bytes 3145736 | tf_op jit(solution)/shard_map/ppermute | solution.py:312
  71.5 2.0 %collective-permute-start.3 = (bf16[4,3,2,64,128]{4,3,2,1,0:T(8,128)(2,1)S(1)}, bf16[4,3,2,64,128]{4,3,2,1,0:T(8,128)(2,1)S(1)}, u32[]{:S(2)}, u32[]{:S(2)}) collective-permute-start(bf16[4,3,2,64,128]{4,3,2,1,0:T(8,128)(2,1)S(1)} %pad_maximum_fusion.4), channel_id=1, source_target_pairs={{0,3},{1,4},{2,5},{3,6},{4,7},{5,8},{6,9},{7,10},{8,11},{9,12},{10... | collective-permute-start | bytes 1179656 | tf_op jit(solution)/shard_map/ppermute | solution.py:178
  74.4 1.9 %collective-permute-start.6 = (bf16[4,4,2,128,128]{4,3,2,1,0:T(8,128)(2,1)}, bf16[4,4,2,128,128]{4,3,2,1,0:T(8,128)(2,1)}, u32[]{:S(2)}, u32[]{:S(2)}) collective-permute-start(bf16[4,4,2,128,128]{4,3,2,1,0:T(8,128)(2,1)} %bitcast.18.refs_0_), channel_id=1, source_target_pairs={{0,64},{64,0},{1,65},{65,1},{2,66},{66,2},{3,67},{67,3},{4,68},{68... | collective-permute-start | bytes 3145736 | tf_op jit(solution)/shard_map/ppermute | solution.py:202
  76.5 8.8 %collective-permute-done.3.refs_2_ = bf16[4,3,2,64,128]{4,3,2,1,0:T(8,128)(2,1)S(1)} collective-permute-done((bf16[4,3,2,64,128]{4,3,2,1,0:T(8,128)(2,1)S(1)}, bf16[4,3,2,64,128]{4,3,2,1,0:T(8,128)(2,1)S(1)}, u32[]{:S(2)}, u32[]{:S(2)}) %collective-permute-start.3) | collective-permute-done | bytes 393248 | tf_op jit(solution)/shard_map/ppermute | solution.py:178
  85.2 3.9 %collective-permute-start.4 = (bf16[4,2,2,64,128]{4,3,2,1,0:T(8,128)(2,1)S(1)}, bf16[4,2,2,64,128]{4,3,2,1,0:T(8,128)(2,1)S(1)}, u32[]{:S(2)}, u32[]{:S(2)}) collective-permute-start(bf16[4,2,2,64,128]{4,3,2,1,0:T(8,128)(2,1)S(1)} %slice.71), channel_id=1, source_target_pairs={{0,3},{1,4},{2,5},{3,6},{4,7},{5,8},{6,9},{7,10},{8,11},{9,12},{10... | collective-permute-start | bytes 786440 | tf_op jit(solution)/shard_map/ppermute | solution.py:178
  89.4 1.3 fusion.bias
  90.7 3.7 %collective-permute-done.4.refs_0_ = bf16[4,2,2,64,128]{4,3,2,1,0:T(8,128)(2,1)S(1)} collective-permute-done((bf16[4,2,2,64,128]{4,3,2,1,0:T(8,128)(2,1)S(1)}, bf16[4,2,2,64,128]{4,3,2,1,0:T(8,128)(2,1)S(1)}, u32[]{:S(2)}, u32[]{:S(2)}) %collective-permute-start.4) | collective-permute-done | bytes 262176 | tf_op jit(solution)/shard_map/ppermute | solution.py:178
  94.5 9.7 %collective-permute-start.5 = (bf16[4,4,2,64,128]{4,3,2,1,0:T(8,128)(2,1)S(1)}, bf16[4,4,2,64,128]{4,3,2,1,0:T(8,128)(2,1)S(1)}, u32[]{:S(2)}, u32[]{:S(2)}) collective-permute-start(bf16[4,4,2,64,128]{4,3,2,1,0:T(8,128)(2,1)S(1)} %pad_maximum_fusion.3), channel_id=1, source_target_pairs={{0,64},{64,0},{1,65},{65,1},{2,66},{66,2},{3,67},{67,3},{4,68},{68... | collective-permute-start | bytes 1572872 | tf_op jit(solution)/shard_map/ppermute | solution.py:313
  105.4 6.8 %shard_map.73 = (f32[4,512,128]{2,1,0:T(8,128)}, f32[4,512,128]{2,1,0:T(8,128)}) custom-call(s32[6]{0:T(128)} %fusion.34.shifts, bf16[4,512,128]{2,1,0:T(8,128)(2,1)} %bitcast.35, f32[4,8,5888]{2,1,0:T(8,128)} %fusion.bias, bf16[4,1,2,64,128]{4,3,2,1,0:T(8,128)(2,1)} %slice.73.refs_0_, bf16[4,4,2,64,128]{4,3,2,1,0:T(8,128)(2,1)} %copy-done.1), custom_call_target="tpu_custom_call" | custom-call | flops 805306368 | bytes 8388608 | tf_op jit(solution)/shard_map/pallas_call | solution.py:134
  112.2 11.7 %shard_map.74 = (f32[4,512,128]{2,1,0:T(8,128)}, f32[4,512,128]{2,1,0:T(8,128)}) custom-call(s32[6]{0:T(128)} %fusion.34.shifts, bf16[4,512,128]{2,1,0:T(8,128)(2,1)} %bitcast.36, f32[4,8,5888]{2,1,0:T(8,128)} %fusion.bias, bf16[4,4,2,64,128]{4,3,2,1,0:T(8,128)(2,1)} %copy-done.2, bf16[4,8,2,64,128]{4,3,2,1,0:T(8,128)(2,1)} %collective-permute-done.7.refs_1_, ...), custom_call_target="tpu_custom_call" | custom-call | flops 1879048192 | bytes 8388608 | tf_op jit(solution)/shard_map/pallas_call | solution.py:134
  123.9 11.6 %shard_map.75 = (f32[4,512,128]{2,1,0:T(8,128)}, f32[4,512,128]{2,1,0:T(8,128)}) custom-call(s32[6]{0:T(128)} %fusion.34.shifts, bf16[4,512,128]{2,1,0:T(8,128)(2,1)} %bitcast.37, f32[4,8,5888]{2,1,0:T(8,128)} %fusion.bias, bf16[4,4,2,128,128]{4,3,2,1,0:T(8,128)(2,1)} %bitcast.18.refs_0_, bf16[4,4,2,128,128]{4,3,2,1,0:T(8,128)(2,1)} %collective-permute-done.6.refs_1_, ...), custom_call_target="tpu_custom_call" | custom-call | flops 1879048192 | bytes 8388608 | tf_op jit(solution)/shard_map/pallas_call | solution.py:134
  135.5 7.1 %shard_map.76 = (f32[4,512,128]{2,1,0:T(8,128)}, f32[4,512,128]{2,1,0:T(8,128)}) custom-call(s32[6]{0:T(128)} %fusion.34.shifts, bf16[4,512,128]{2,1,0:T(8,128)(2,1)} %bitcast.38, f32[4,8,5888]{2,1,0:T(8,128)} %fusion.bias, bf16[4,2,2,64,128]{4,3,2,1,0:T(8,128)(2,1)} %copy-done.4, f32[4,512,128]{2,1,0:T(8,128)} %get-tuple-element.21.refs_1_, ...), custom_call_target="tpu_custom_call" | custom-call | flops 536870912 | bytes 8388608 | tf_op jit(solution)/shard_map/pallas_call | solution.py:134
  142.7 0.8 copy-done.5
  143.5 8.6 %shard_map.77 = bf16[4,512,128]{2,1,0:T(8,128)(2,1)} custom-call(s32[6]{0:T(128)} %fusion.34.shifts, bf16[4,512,128]{2,1,0:T(8,128)(2,1)} %bitcast.39, f32[4,8,5888]{2,1,0:T(8,128)} %fusion.bias, bf16[4,4,2,64,128]{4,3,2,1,0:T(8,128)(2,1)} %copy-done.5, f32[4,512,128]{2,1,0:T(8,128)} %get-tuple-element.23.refs_1_, f32[4,512,128]{2,1,0:T(8,128)} %get-tuple-element.24.refs_2_), custom_call_target="tpu_custom_call" | custom-call | flops 1073741824 | bytes 8388608 | tf_op jit(solution)/shard_map/pallas_call | solution.py:134
  152.1 17.7 %all_to_all.20 = bf16[16,128,128]{2,1,0:T(8,128)(2,1)S(1)} all-to-all(bf16[16,128,128]{2,1,0:T(8,128)(2,1)} %bitcast.40), channel_id=1, replica_groups=mesh['y'=4,'core'=2,'x'=4,'z'=16] {'x','y'}, dimensions={0} | all-to-all | bytes 1048576 | tf_op jit(solution)/shard_map/all_to_all | solution.py:173
  169.7 1.1 copy.30
  (83 shorter events, 7.3 us)
Async XLA Ops:
  4.8 10.3 %collective-permute-start = (bf16[16,2,64,128]{3,2,1,0:T(8,128)(2,1)S(1)}, bf16[16,2,64,128]{3,2,1,0:T(8,128)(2,1)S(1)}, u32[]{:S(2)}, u32[]{:S(2)}) collective-permute-start(bf16[16,2,64,128]{3,2,1,0:T(8,128)(2,1)S(1)} %fusion.2), channel_id=1, source_target_pairs={{0,64},{64,0},{1,65},{65,1},{2,66},{66,2},{3,67},{67,3},{4,68},{68... | collective-permute-start | bytes 1572872 | tf_op jit(solution)/shard_map/ppermute | solution.py:184
  16.1 13.7 %all-to-all-start = ((bf16[16,2,64,128]{3,2,1,0:T(8,128)(2,1)}), bf16[16,2,64,128]{3,2,1,0:T(8,128)(2,1)S(1)}, u32[]{:S(2)}, u32[]{:S(2)}) async-start(bf16[16,2,64,128]{3,2,1,0:T(8,128)(2,1)} %broadcast_select_fusion), calls=%async_computation | async-start | bytes 1048576 | tf_op jit(solution)/shard_map/all_to_all | solution.py:173
  19.8 20.0 %copy-start.18 = (s32[1,92]{1,0:T(1,128)S(1)}, s32[1,92]{1,0:T(1,128)}, u32[]{:S(2)}) copy-start(s32[1,92]{1,0:T(1,128)} %constant.218) | copy-start | bytes 1108
  19.8 20.0 %copy-start.19 = (s32[1,92]{1,0:T(1,128)S(1)}, s32[1,92]{1,0:T(1,128)}, u32[]{:S(2)}) copy-start(s32[1,92]{1,0:T(1,128)} %constant.224) | copy-start | bytes 1108
  19.8 20.0 %copy-start.6 = (bf16[128,16,128]{2,1,0:T(8,128)(2,1)S(1)}, bf16[128,16,128]{2,1,0:T(8,128)(2,1)}, u32[]{:S(2)}) copy-start(bf16[128,16,128]{2,1,0:T(8,128)(2,1)} %param.7) | copy-start | bytes 1572868
  30.5 10.3 %copy-start.8 = (s32[64]{0:T(128)S(1)}, s32[64]{0:T(128)}, u32[]{:S(2)}) copy-start(s32[64]{0:T(128)} %param.11) | copy-start | bytes 772
  30.6 17.7 %collective-permute-start.1 = (bf16[4,4,2,64,128]{4,3,2,1,0:T(8,128)(2,1)S(1)}, bf16[4,4,2,64,128]{4,3,2,1,0:T(8,128)(2,1)S(1)}, u32[]{:S(2)}, u32[]{:S(2)}) collective-permute-start(bf16[4,4,2,64,128]{4,3,2,1,0:T(8,128)(2,1)S(1)} %broadcast_select_fusion.1), channel_id=1, source_target_pairs={{0,1},{1,2},{2,3},{3,4},{4,5},{5,6},{6,7},{7,8},{8,9},{9,10},{10,1... | collective-permute-start | bytes 1572872 | tf_op jit(solution)/shard_map/ppermute | solution.py:178
  39.8 5.4 %copy-start.13 = (s32[1,92]{1,0:T(1,128)S(1)}, s32[1,92]{1,0:T(1,128)}, u32[]{:S(2)}) copy-start(s32[1,92]{1,0:T(1,128)} %constant.214) | copy-start | bytes 1108
  39.8 5.4 %copy-start.14 = (pred[1,92]{1,0:T(4,128)(4,1)S(1)}, pred[1,92]{1,0:T(4,128)(4,1)}, u32[]{:S(2)}) copy-start(pred[1,92]{1,0:T(4,128)(4,1)} %constant.215) | copy-start | bytes 280
  39.8 5.4 %copy-start.15 = (pred[1,92]{1,0:T(4,128)(4,1)S(1)}, pred[1,92]{1,0:T(4,128)(4,1)}, u32[]{:S(2)}) copy-start(pred[1,92]{1,0:T(4,128)(4,1)} %constant.216) | copy-start | bytes 280
  41.4 12.7 %all-to-all-start.1 = ((bf16[16,128,128]{2,1,0:T(8,128)(2,1)}), bf16[16,128,128]{2,1,0:T(8,128)(2,1)S(1)}, u32[]{:S(2)}, u32[]{:S(2)}) async-start(bf16[16,128,128]{2,1,0:T(8,128)(2,1)} %bitcast.34), calls=%async_computation.1 | async-start | bytes 1048576 | tf_op jit(solution)/shard_map/all_to_all | solution.py:173
  48.3 3.2 %copy-start.16 = (s32[1,92]{1,0:T(1,128)S(1)}, s32[1,92]{1,0:T(1,128)}, u32[]{:S(2)}) copy-start(s32[1,92]{1,0:T(1,128)} %constant.213) | copy-start | bytes 1108
  48.3 3.2 %copy-start.17 = (s32[1,92]{1,0:T(1,128)S(1)}, s32[1,92]{1,0:T(1,128)}, u32[]{:S(2)}) copy-start(s32[1,92]{1,0:T(1,128)} %constant.217) | copy-start | bytes 1108
  48.3 14.8 %copy-start.1 = (bf16[4,4,2,64,128]{4,3,2,1,0:T(8,128)(2,1)}, bf16[4,4,2,64,128]{4,3,2,1,0:T(8,128)(2,1)S(1)}, u32[]{:S(2)}) copy-start(bf16[4,4,2,64,128]{4,3,2,1,0:T(8,128)(2,1)S(1)} %collective-permute-done.1.refs_1_) | copy-start | bytes 1572868
  48.4 14.7 %collective-permute-start.2 = (bf16[4,4,2,64,128]{4,3,2,1,0:T(8,128)(2,1)S(1)}, bf16[4,4,2,64,128]{4,3,2,1,0:T(8,128)(2,1)S(1)}, u32[]{:S(2)}, u32[]{:S(2)}) collective-permute-start(bf16[4,4,2,64,128]{4,3,2,1,0:T(8,128)(2,1)S(1)} %pad_maximum_fusion.2), channel_id=1, source_target_pairs={{0,2},{1,3},{2,4},{3,5},{4,6},{5,7},{6,8},{7,9},{8,10},{9,11},{10,... | collective-permute-start | bytes 1572872 | tf_op jit(solution)/shard_map/ppermute | solution.py:178
  51.5 7.8 %copy-start.7 = (s32[64,16,16]{0,2,1:T(8,128)S(1)}, s32[64,16,16]{0,2,1:T(8,128)}, u32[]{:S(2)}) copy-start(s32[64,16,16]{0,2,1:T(8,128)} %param.10) | copy-start | bytes 196612
  51.5 8.0 %copy-start.9 = (pred[92]{0:T(512)(128)(4,1)S(1)}, pred[92]{0:T(512)(128)(4,1)}, u32[]{:S(2)}) copy-start(pred[92]{0:T(512)(128)(4,1)} %constant.210) | copy-start | bytes 280
  54.1 0.8 copy-start
  54.9 19.5 %all-to-all-start.2 = ((bf16[16,2,128,128]{3,2,1,0:T(8,128)(2,1)}), bf16[16,2,128,128]{3,2,1,0:T(8,128)(2,1)}, u32[]{:S(2)}, u32[]{:S(2)}) async-start(bf16[16,2,128,128]{3,2,1,0:T(8,128)(2,1)} %pad_maximum_fusion), calls=%async_computation.2 | async-start | bytes 2097152 | tf_op jit(solution)/shard_map/all_to_all | solution.py:173
  63.1 8.3 %copy-start.2 = (bf16[4,4,2,64,128]{4,3,2,1,0:T(8,128)(2,1)}, bf16[4,4,2,64,128]{4,3,2,1,0:T(8,128)(2,1)S(1)}, u32[]{:S(2)}) copy-start(bf16[4,4,2,64,128]{4,3,2,1,0:T(8,128)(2,1)S(1)} %collective-permute-done.2.refs_0_) | copy-start | bytes 1572868
  64.3 48.0 %collective-permute-start.7 = (bf16[4,8,2,64,128]{4,3,2,1,0:T(8,128)(2,1)}, bf16[4,8,2,64,128]{4,3,2,1,0:T(8,128)(2,1)}, u32[]{:S(2)}, u32[]{:S(2)}) collective-permute-start(bf16[4,8,2,64,128]{4,3,2,1,0:T(8,128)(2,1)} %pad_maximum_fusion.1), channel_id=1, source_target_pairs={{0,64},{64,0},{1,65},{65,1},{2,66},{66,2},{3,67},{67,3},{4,68},{68... | collective-permute-start | bytes 3145736 | tf_op jit(solution)/shard_map/ppermute | solution.py:312
  71.4 5.0 %copy-start.10 = (pred[92]{0:T(512)(128)(4,1)S(1)}, pred[92]{0:T(512)(128)(4,1)}, u32[]{:S(2)}) copy-start(pred[92]{0:T(512)(128)(4,1)} %constant.220) | copy-start | bytes 280
  71.4 5.0 %copy-start.11 = (pred[92]{0:T(512)(128)(4,1)S(1)}, pred[92]{0:T(512)(128)(4,1)}, u32[]{:S(2)}) copy-start(pred[92]{0:T(512)(128)(4,1)} %constant.222) | copy-start | bytes 280
  71.4 5.0 %copy-start.12 = (s32[92]{0:T(128)S(1)}, s32[92]{0:T(128)}, u32[]{:S(2)}) copy-start(s32[92]{0:T(128)} %constant.223) | copy-start | bytes 1108
  71.5 13.8 %collective-permute-start.3 = (bf16[4,3,2,64,128]{4,3,2,1,0:T(8,128)(2,1)S(1)}, bf16[4,3,2,64,128]{4,3,2,1,0:T(8,128)(2,1)S(1)}, u32[]{:S(2)}, u32[]{:S(2)}) collective-permute-start(bf16[4,3,2,64,128]{4,3,2,1,0:T(8,128)(2,1)S(1)} %pad_maximum_fusion.4), channel_id=1, source_target_pairs={{0,3},{1,4},{2,5},{3,6},{4,7},{5,8},{6,9},{7,10},{8,11},{9,12},{10... | collective-permute-start | bytes 1179656 | tf_op jit(solution)/shard_map/ppermute | solution.py:178
  74.4 49.5 %collective-permute-start.6 = (bf16[4,4,2,128,128]{4,3,2,1,0:T(8,128)(2,1)}, bf16[4,4,2,128,128]{4,3,2,1,0:T(8,128)(2,1)}, u32[]{:S(2)}, u32[]{:S(2)}) collective-permute-start(bf16[4,4,2,128,128]{4,3,2,1,0:T(8,128)(2,1)} %bitcast.18.refs_0_), channel_id=1, source_target_pairs={{0,64},{64,0},{1,65},{65,1},{2,66},{66,2},{3,67},{67,3},{4,68},{68... | collective-permute-start | bytes 3145736 | tf_op jit(solution)/shard_map/ppermute | solution.py:202
  85.2 9.3 %copy-start.3 = (bf16[4,3,2,64,128]{4,3,2,1,0:T(8,128)(2,1)}, bf16[4,3,2,64,128]{4,3,2,1,0:T(8,128)(2,1)S(1)}, u32[]{:S(2)}) copy-start(bf16[4,3,2,64,128]{4,3,2,1,0:T(8,128)(2,1)S(1)} %collective-permute-done.3.refs_2_) | copy-start | bytes 1179652
  85.2 9.2 %collective-permute-start.4 = (bf16[4,2,2,64,128]{4,3,2,1,0:T(8,128)(2,1)S(1)}, bf16[4,2,2,64,128]{4,3,2,1,0:T(8,128)(2,1)S(1)}, u32[]{:S(2)}, u32[]{:S(2)}) collective-permute-start(bf16[4,2,2,64,128]{4,3,2,1,0:T(8,128)(2,1)S(1)} %slice.71), channel_id=1, source_target_pairs={{0,3},{1,4},{2,5},{3,6},{4,7},{5,8},{6,9},{7,10},{8,11},{9,12},{10... | collective-permute-start | bytes 786440 | tf_op jit(solution)/shard_map/ppermute | solution.py:178
  94.4 17.8 %copy-start.4 = (bf16[4,2,2,64,128]{4,3,2,1,0:T(8,128)(2,1)}, bf16[4,2,2,64,128]{4,3,2,1,0:T(8,128)(2,1)S(1)}, u32[]{:S(2)}) copy-start(bf16[4,2,2,64,128]{4,3,2,1,0:T(8,128)(2,1)S(1)} %collective-permute-done.4.refs_0_) | copy-start | bytes 786436
  94.5 48.1 %collective-permute-start.5 = (bf16[4,4,2,64,128]{4,3,2,1,0:T(8,128)(2,1)S(1)}, bf16[4,4,2,64,128]{4,3,2,1,0:T(8,128)(2,1)S(1)}, u32[]{:S(2)}, u32[]{:S(2)}) collective-permute-start(bf16[4,4,2,64,128]{4,3,2,1,0:T(8,128)(2,1)S(1)} %pad_maximum_fusion.3), channel_id=1, source_target_pairs={{0,64},{64,0},{1,65},{65,1},{2,66},{66,2},{3,67},{67,3},{4,68},{68... | collective-permute-start | bytes 1572872 | tf_op jit(solution)/shard_map/ppermute | solution.py:313
  142.7 0.8 copy-start.5

commit v4 on v3

--- a/solution.py
+++ b/solution.py
@@ -193,7 +193,7 @@
     parts = parts * 2 - 3 * (parts // 2)
     row_y = (own_anchors[:, None] // 4 + parts[None, :]) % 4
     index = (slot_ids[:, None] * rows_y + row_y).reshape(-1)
-    held = jnp.take(block, index, axis=0).reshape(planes, 4, 2, block_rows, head_dim)
+    held = jnp.take(block, index, axis=0, mode="clip").reshape(planes, 4, 2, block_rows, head_dim)
 
     head_queries = spread(after(jnp.transpose(queries, (1, 0, 2)), held))
     own_pair = spread(after(packed, head_queries))
@@ -260,16 +260,14 @@
     begin()
     own(0, 0)
     own(1, 1)
-    for entry in range(3):
-        anchor(2, entry, 1, 4 + entry)
+    for which, side in ((2, 1), (3, -1)):
+        for entry in range(3):
+            anchor(which, entry, side, 4 + entry)
     end()
     begin()
-    for entry in range(2):
-        anchor(0, entry, 1, 7 + entry)
-    end()
-    begin()
-    for entry in range(4):
-        anchor(0, entry, -1, 4 + entry)
+    anchor(0, 0, 1, 7)
+    anchor(0, 1, 1, 8)
+    anchor(1, 0, -1, 7)
     end()
 
     table = jnp.asarray(np.array(entries, np.int32).T)
@@ -310,14 +308,12 @@
     )
     fourth = onward(third[:, :2], 3)
     near_other = lax.ppermute(jnp.concatenate([first, second], axis=1), "core", swap)
-    far_other = lax.ppermute(
-        jnp.concatenate([third, fourth[:, :1]], axis=1), "core", swap
-    )
-    state = run(0, [held[:, :1], first], None)
+    third_other = lax.ppermute(third, "core", swap)
+    fourth_other = lax.ppermute(fourth[:, :1], "core", swap)
+    state = run(0, [held, first], None)
     state = run(1, [second, near_other], state)
-    state = run(2, [own_pair, partner_pair, third], state)
-    state = run(3, [fourth], state)
-    state = run(4, [far_other], state, last=True)
+    state = run(2, [own_pair, partner_pair, third, third_other], state)
+    state = run(3, [fourth, fourth_other], state, last=True)
 
     output = state[0].reshape(planes * rows_y, local_rows, head_dim)
     return jnp.transpose(spread(output), (1, 0, 2))

time: 172 us -> 170 us (0.988)
  Pallas kernels: 45.8 us -> 40.3 us
  starting transfers between devices: 57.2 us -> 61.8 us
  waiting for transfers between devices: 29.4 us -> 31.2 us
    ppermute x4, starting transfers between devices: 18.2 us -> 30.3 us  [onward(): return lax.ppermute(carried, ('core', 'z'), route)]
    pallas_call x5 -> x4, Pallas kernels: 45.8 us -> 40.3 us  [attend(): pl.pallas_call(functools.partial(attend_kernel, plan, state is None, last...]
    ppermute x1 -> x2, starting transfers between devices: 9.68 us -> 4.33 us  [the longest x1 2.41 us: local(): fourth_other = lax.ppermute(fourth[:, :1], 'core', swap)]
    all_to_all x3, waiting for transfers between devices: 12.6 us -> 17.7 us  [spread(): lax.all_to_all(packed, ('x', 'y'), split_axis=0, concat_axis=0, tiled=True)]
    ppermute x1, starting transfers between devices: 7.04 us -> 4.52 us  [local(): lax.ppermute(jnp.concatenate([first, second], axis=1), 'core', swap)]
    ppermute x4, waiting for transfers between devices: 15.9 us -> 13.5 us  [onward(): return lax.ppermute(carried, ('core', 'z'), route)]
  transfers between devices with their start and end apart: 11 -> 12, of which waited for: 6 -> 4; matrix products, arithmetic and copies ran while one was open for 6% -> 5% of each run, Pallas kernels for 22% -> 19%
where the time goes in v4:
time: 170 us; the launch traced here: 169 us
  starting transfers between devices  61.8 us (36%)
  Pallas kernels  40.3 us (24%)
  waiting for transfers between devices  31.2 us (18%)
  blocking collectives  16.9 us (10%)
  local copies, waits for them, and re-layouts  8.67 us (5%)
  other arithmetic  6.26 us (4%)
  between operations  2.53 us (1%)
    pallas_call x4, Pallas kernels, attend(): pl.pallas_call(functools.partial(attend_kernel, plan, state is None, last...  40.3 us
    ppermute x4, starting transfers between devices, onward(): return lax.ppermute(carried, ('core', 'z'), route)  30.3 us
    all_to_all x3, waiting for transfers between devices, spread(): lax.all_to_all(packed, ('x', 'y'), split_axis=0, concat_axis=0, tiled=True)  17.7 us
    all_to_all x1, blocking collectives, spread(): lax.all_to_all(packed, ('x', 'y'), split_axis=0, concat_axis=0, tiled=True)  16.9 us
    ppermute x4, waiting for transfers between devices, onward(): return lax.ppermute(carried, ('core', 'z'), route)  13.5 us
    all_to_all x3, starting transfers between devices, spread(): lax.all_to_all(packed, ('x', 'y'), split_axis=0, concat_axis=0, tiled=True)  11.8 us
    ppermute x1, starting transfers between devices, local(): lax.ppermute(block, 'core', swap)  8.88 us
    ppermute x1, starting transfers between devices, local(): lax.ppermute(jnp.concatenate([first, second], axis=1), 'core', swap)  4.52 us
  transfers between devices with their start and end apart: 12, of which 4 were waited for; matrix products, arithmetic and copies ran while one was open for 5% of the time, Pallas kernels for 19%

profile of v4, /device:TPU:1, one launch (start us, length us, event | category | flops | bytes accessed | tf_op | source)
XLA Modules:
  0.0 169.0 jit_solution(12278272660210229837)
XLA Ops:
  0.0 0.7 and_select_fusion.4
  3.2 1.5 copy_bitcast_fusion
  4.8 8.9 %collective-permute-start = (bf16[16,2,64,128]{3,2,1,0:T(8,128)(2,1)S(1)}, bf16[16,2,64,128]{3,2,1,0:T(8,128)(2,1)S(1)}, u32[]{:S(2)}, u32[]{:S(2)}) collective-permute-start(bf16[16,2,64,128]{3,2,1,0:T(8,128)(2,1)S(1)} %fusion.2), channel_id=1, source_target_pairs={{0,64},{64,0},{1,65},{65,1},{2,66},{66,2},{3,67},{67,3},{4,68},{68... | collective-permute-start | bytes 1572872 | tf_op jit(solution)/shard_map/ppermute | solution.py:184
  14.3 0.9 copy.34
  15.2 1.0 broadcast_select_fusion
  16.2 3.7 %all-to-all-start = ((bf16[16,2,64,128]{3,2,1,0:T(8,128)(2,1)}), bf16[16,2,64,128]{3,2,1,0:T(8,128)(2,1)S(1)}, u32[]{:S(2)}, u32[]{:S(2)}) async-start(bf16[16,2,64,128]{3,2,1,0:T(8,128)(2,1)} %broadcast_select_fusion), calls=%async_computation | async-start | bytes 1048576 | tf_op jit(solution)/shard_map/all_to_all | solution.py:173
  20.0 10.0 %all-to-all-done = bf16[16,2,64,128]{3,2,1,0:T(8,128)(2,1)S(1)} async-done(((bf16[16,2,64,128]{3,2,1,0:T(8,128)(2,1)}), bf16[16,2,64,128]{3,2,1,0:T(8,128)(2,1)S(1)}, u32[]{:S(2)}, u32[]{:S(2)}) %all-to-all-start) | async-done | bytes 524320 | tf_op jit(solution)/shard_map/all_to_all | solution.py:173
  30.1 0.6 gather_fusion
  30.7 9.2 %collective-permute-start.1 = (bf16[4,4,2,64,128]{4,3,2,1,0:T(8,128)(2,1)S(1)}, bf16[4,4,2,64,128]{4,3,2,1,0:T(8,128)(2,1)S(1)}, u32[]{:S(2)}, u32[]{:S(2)}) collective-permute-start(bf16[4,4,2,64,128]{4,3,2,1,0:T(8,128)(2,1)S(1)} %bitcast.41), channel_id=1, source_target_pairs={{0,1},{1,2},{2,3},{3,4},{4,5},{5,6},{6,7},{7,8},{8,9},{9,10},{10,1... | collective-permute-start | bytes 1572872 | tf_op jit(solution)/shard_map/ppermute | solution.py:178
  40.0 3.8 %all-to-all-start.1 = ((bf16[16,128,128]{2,1,0:T(8,128)(2,1)}), bf16[16,128,128]{2,1,0:T(8,128)(2,1)S(1)}, u32[]{:S(2)}, u32[]{:S(2)}) async-start(bf16[16,128,128]{2,1,0:T(8,128)(2,1)} %bitcast.34), calls=%async_computation.1 | async-start | bytes 1048576 | tf_op jit(solution)/shard_map/all_to_all | solution.py:173
  43.9 1.1 pad_maximum_fusion
  45.1 7.6 %all-to-all-done.1 = bf16[16,128,128]{2,1,0:T(8,128)(2,1)S(1)} async-done(((bf16[16,128,128]{2,1,0:T(8,128)(2,1)}), bf16[16,128,128]{2,1,0:T(8,128)(2,1)S(1)}, u32[]{:S(2)}, u32[]{:S(2)}) %all-to-all-start.1) | async-done | bytes 524320 | tf_op jit(solution)/shard_map/all_to_all | solution.py:173
  52.7 4.3 %all-to-all-start.2 = ((bf16[16,2,128,128]{3,2,1,0:T(8,128)(2,1)}), bf16[16,2,128,128]{3,2,1,0:T(8,128)(2,1)}, u32[]{:S(2)}, u32[]{:S(2)}) async-start(bf16[16,2,128,128]{3,2,1,0:T(8,128)(2,1)} %pad_maximum_fusion), calls=%async_computation.2 | async-start | bytes 2097152 | tf_op jit(solution)/shard_map/all_to_all | solution.py:173
  57.2 3.3 %collective-permute-start.2 = (bf16[4,4,2,64,128]{4,3,2,1,0:T(8,128)(2,1)S(1)}, bf16[4,4,2,64,128]{4,3,2,1,0:T(8,128)(2,1)S(1)}, u32[]{:S(2)}, u32[]{:S(2)}) collective-permute-start(bf16[4,4,2,64,128]{4,3,2,1,0:T(8,128)(2,1)S(1)} %pad_maximum_fusion.2), channel_id=1, source_target_pairs={{0,2},{1,3},{2,4},{3,5},{4,6},{5,7},{6,8},{7,9},{8,10},{9,11},{10,... | collective-permute-start | bytes 1572872 | tf_op jit(solution)/shard_map/ppermute | solution.py:178
  60.6 0.7 fusion.34
  61.3 2.1 %compare_bitcast_fusion = pred[92]{0:T(512)(128)(4,1)S(1)} fusion(s32[1,92]{1,0:T(1,128)S(1)} %copy-done.14, pred[1,92]{1,0:T(4,128)(4,1)S(1)} %copy-done.15, pred[1,92]{1,0:T(4,128)(4,1)S(1)} %copy-done.16, s32[]{:T(128)} %bitcast.14, s32[]{:T(128)} %bitcast.13, s32[]{:T(128)} %bitcast.12), kind=kLoop, calls=%fused_computation.52 | loop fusion | flops 1196 | bytes 656 | tf_op jit(solution)/shard_map/and | solution.py:280
  63.4 7.9 %collective-permute-done.2.refs_0_ = bf16[4,4,2,64,128]{4,3,2,1,0:T(8,128)(2,1)S(1)} collective-permute-done((bf16[4,4,2,64,128]{4,3,2,1,0:T(8,128)(2,1)S(1)}, bf16[4,4,2,64,128]{4,3,2,1,0:T(8,128)(2,1)S(1)}, u32[]{:S(2)}, u32[]{:S(2)}) %collective-permute-start.2) | collective-permute-done | bytes 524320 | tf_op jit(solution)/shard_map/ppermute | solution.py:178
  71.5 4.5 %collective-permute-start.8 = (bf16[4,8,2,64,128]{4,3,2,1,0:T(8,128)(2,1)S(1)}, bf16[4,8,2,64,128]{4,3,2,1,0:T(8,128)(2,1)}, u32[]{:S(2)}, u32[]{:S(2)}) collective-permute-start(bf16[4,8,2,64,128]{4,3,2,1,0:T(8,128)(2,1)S(1)} %pad_maximum_fusion.1), channel_id=1, source_target_pairs={{0,64},{64,0},{1,65},{65,1},{2,66},{66,2},{3,67},{67,3},{4,68},{68... | collective-permute-start | bytes 3145736 | tf_op jit(solution)/shard_map/ppermute | solution.py:310
  76.1 7.8 %collective-permute-start.3 = (bf16[4,3,2,64,128]{4,3,2,1,0:T(8,128)(2,1)S(1)}, bf16[4,3,2,64,128]{4,3,2,1,0:T(8,128)(2,1)S(1)}, u32[]{:S(2)}, u32[]{:S(2)}) collective-permute-start(bf16[4,3,2,64,128]{4,3,2,1,0:T(8,128)(2,1)S(1)} %pad_maximum_fusion.3), channel_id=1, source_target_pairs={{0,3},{1,4},{2,5},{3,6},{4,7},{5,8},{6,9},{7,10},{8,11},{9,12},{10... | collective-permute-start | bytes 1179656 | tf_op jit(solution)/shard_map/ppermute | solution.py:178
  83.9 1.9 %collective-permute-start.6 = (bf16[4,4,2,128,128]{4,3,2,1,0:T(8,128)(2,1)}, bf16[4,4,2,128,128]{4,3,2,1,0:T(8,128)(2,1)}, u32[]{:S(2)}, u32[]{:S(2)}) collective-permute-start(bf16[4,4,2,128,128]{4,3,2,1,0:T(8,128)(2,1)} %bitcast.18.refs_0_), channel_id=1, source_target_pairs={{0,64},{64,0},{1,65},{65,1},{2,66},{66,2},{3,67},{67,3},{4,68},{68... | collective-permute-start | bytes 3145736 | tf_op jit(solution)/shard_map/ppermute | solution.py:202
  87.3 5.6 %collective-permute-done.3.refs_2_ = bf16[4,3,2,64,128]{4,3,2,1,0:T(8,128)(2,1)S(1)} collective-permute-done((bf16[4,3,2,64,128]{4,3,2,1,0:T(8,128)(2,1)S(1)}, bf16[4,3,2,64,128]{4,3,2,1,0:T(8,128)(2,1)S(1)}, u32[]{:S(2)}, u32[]{:S(2)}) %collective-permute-start.3) | collective-permute-done | bytes 393248 | tf_op jit(solution)/shard_map/ppermute | solution.py:178
  92.9 9.9 %collective-permute-start.4 = (bf16[4,2,2,64,128]{4,3,2,1,0:T(8,128)(2,1)S(1)}, bf16[4,2,2,64,128]{4,3,2,1,0:T(8,128)(2,1)S(1)}, u32[]{:S(2)}, u32[]{:S(2)}) collective-permute-start(bf16[4,2,2,64,128]{4,3,2,1,0:T(8,128)(2,1)S(1)} %slice.67), channel_id=1, source_target_pairs={{0,3},{1,4},{2,5},{3,6},{4,7},{5,8},{6,9},{7,10},{8,11},{9,12},{10... | collective-permute-start | bytes 786440 | tf_op jit(solution)/shard_map/ppermute | solution.py:178
  102.8 1.9 %collective-permute-start.7 = (bf16[4,3,2,64,128]{4,3,2,1,0:T(8,128)(2,1)S(1)}, bf16[4,3,2,64,128]{4,3,2,1,0:T(8,128)(2,1)S(1)}, u32[]{:S(2)}, u32[]{:S(2)}) collective-permute-start(bf16[4,3,2,64,128]{4,3,2,1,0:T(8,128)(2,1)S(1)} %collective-permute-done.3.refs_2_), channel_id=1, source_target_pairs={{0,64},{64,0},{1,65},{65,1},{2,66},{66,2},{3,67},{67,3},{4,68},{68... | collective-permute-start | bytes 1179656 | tf_op jit(solution)/shard_map/ppermute | solution.py:311
  104.8 1.3 fusion.bias
  106.7 6.9 %shard_map.73 = (f32[4,512,128]{2,1,0:T(8,128)}, f32[4,512,128]{2,1,0:T(8,128)}) custom-call(s32[6]{0:T(128)} %fusion.31.shifts, bf16[4,512,128]{2,1,0:T(8,128)(2,1)} %bitcast.35, f32[4,8,5888]{2,1,0:T(8,128)} %fusion.bias, bf16[4,4,2,64,128]{4,3,2,1,0:T(8,128)(2,1)} %bitcast.43, bf16[4,4,2,64,128]{4,3,2,1,0:T(8,128)(2,1)} %copy-done.1), custom_call_target="tpu_custom_call" | custom-call | flops 805306368 | bytes 8388608 | tf_op jit(solution)/shard_map/pallas_call | solution.py:134
  113.6 2.4 %collective-permute-start.5 = (bf16[4,1,2,64,128]{4,3,2,1,0:T(8,128)(2,1)S(1)}, bf16[4,1,2,64,128]{4,3,2,1,0:T(8,128)(2,1)S(1)}, u32[]{:S(2)}, u32[]{:S(2)}) collective-permute-start(bf16[4,1,2,64,128]{4,3,2,1,0:T(8,128)(2,1)S(1)} %slice.68), channel_id=1, source_target_pairs={{0,64},{64,0},{1,65},{65,1},{2,66},{66,2},{3,67},{67,3},{4,68},{68... | collective-permute-start | bytes 393224 | tf_op jit(solution)/shard_map/ppermute | solution.py:312
  116.1 11.7 %shard_map.74 = (f32[4,512,128]{2,1,0:T(8,128)}, f32[4,512,128]{2,1,0:T(8,128)}) custom-call(s32[6]{0:T(128)} %fusion.31.shifts, bf16[4,512,128]{2,1,0:T(8,128)(2,1)} %bitcast.36, f32[4,8,5888]{2,1,0:T(8,128)} %fusion.bias, bf16[4,4,2,64,128]{4,3,2,1,0:T(8,128)(2,1)} %copy-done.3, bf16[4,8,2,64,128]{4,3,2,1,0:T(8,128)(2,1)} %collective-permute-done.8.refs_1_, ...), custom_call_target="tpu_custom_call" | custom-call | flops 1879048192 | bytes 8388608 | tf_op jit(solution)/shard_map/pallas_call | solution.py:134
  127.8 0.8 copy-done.21
  128.5 13.7 %shard_map.75 = (f32[4,512,128]{2,1,0:T(8,128)}, f32[4,512,128]{2,1,0:T(8,128)}) custom-call(s32[6]{0:T(128)} %fusion.31.shifts, bf16[4,512,128]{2,1,0:T(8,128)(2,1)} %bitcast.37, f32[4,8,5888]{2,1,0:T(8,128)} %fusion.bias, bf16[4,4,2,128,128]{4,3,2,1,0:T(8,128)(2,1)} %bitcast.18.refs_0_, bf16[4,4,2,128,128]{4,3,2,1,0:T(8,128)(2,1)} %collective-permute-done.6.refs_1_, ...), custom_call_target="tpu_custom_call" | custom-call | flops 2684354560 | bytes 8388608 | tf_op jit(solution)/shard_map/pallas_call | solution.py:134
  142.9 8.0 %shard_map.76 = bf16[4,512,128]{2,1,0:T(8,128)(2,1)} custom-call(s32[6]{0:T(128)} %fusion.31.shifts, bf16[4,512,128]{2,1,0:T(8,128)(2,1)} %bitcast.38, f32[4,8,5888]{2,1,0:T(8,128)} %fusion.bias, bf16[4,2,2,64,128]{4,3,2,1,0:T(8,128)(2,1)} %copy-done.4, bf16[4,1,2,64,128]{4,3,2,1,0:T(8,128)(2,1)} %copy-done.8, f32[4,512,128]{2,1,0:T(8,128)} %get-tuple-element.19.refs_2_, ...), custom_call_target="tpu_custom_call" | custom-call | flops 805306368 | bytes 8388608 | tf_op jit(solution)/shard_map/pallas_call | solution.py:134
  150.9 16.9 %all_to_all.20 = bf16[16,128,128]{2,1,0:T(8,128)(2,1)S(1)} all-to-all(bf16[16,128,128]{2,1,0:T(8,128)(2,1)} %bitcast.39), channel_id=1, replica_groups=mesh['y'=4,'core'=2,'x'=4,'z'=16] {'x','y'}, dimensions={0} | all-to-all | bytes 1048576 | tf_op jit(solution)/shard_map/all_to_all | solution.py:173
  167.9 1.1 copy.30
  (85 shorter events, 4.5 us)
Async XLA Ops:
  4.7 9.6 %copy-start.5 = (bf16[128,16,128]{2,1,0:T(8,128)(2,1)S(1)}, bf16[128,16,128]{2,1,0:T(8,128)(2,1)}, u32[]{:S(2)}) copy-start(bf16[128,16,128]{2,1,0:T(8,128)(2,1)} %param.7) | copy-start | bytes 1572868
  4.8 10.4 %collective-permute-start = (bf16[16,2,64,128]{3,2,1,0:T(8,128)(2,1)S(1)}, bf16[16,2,64,128]{3,2,1,0:T(8,128)(2,1)S(1)}, u32[]{:S(2)}, u32[]{:S(2)}) collective-permute-start(bf16[16,2,64,128]{3,2,1,0:T(8,128)(2,1)S(1)} %fusion.2), channel_id=1, source_target_pairs={{0,64},{64,0},{1,65},{65,1},{2,66},{66,2},{3,67},{67,3},{4,68},{68... | collective-permute-start | bytes 1572872 | tf_op jit(solution)/shard_map/ppermute | solution.py:184
  16.2 3.7 %copy-start.19 = (s32[1,92]{1,0:T(1,128)S(1)}, s32[1,92]{1,0:T(1,128)}, u32[]{:S(2)}) copy-start(s32[1,92]{1,0:T(1,128)} %constant.203) | copy-start | bytes 1108
  16.2 3.8 %copy-start.20 = (s32[1,92]{1,0:T(1,128)S(1)}, s32[1,92]{1,0:T(1,128)}, u32[]{:S(2)}) copy-start(s32[1,92]{1,0:T(1,128)} %constant.209) | copy-start | bytes 1108
  16.2 13.8 %all-to-all-start = ((bf16[16,2,64,128]{3,2,1,0:T(8,128)(2,1)}), bf16[16,2,64,128]{3,2,1,0:T(8,128)(2,1)S(1)}, u32[]{:S(2)}, u32[]{:S(2)}) async-start(bf16[16,2,64,128]{3,2,1,0:T(8,128)(2,1)} %broadcast_select_fusion), calls=%async_computation | async-start | bytes 1048576 | tf_op jit(solution)/shard_map/all_to_all | solution.py:173
  20.0 23.7 %copy-start.10 = (pred[92]{0:T(512)(128)(4,1)S(1)}, pred[92]{0:T(512)(128)(4,1)}, u32[]{:S(2)}) copy-start(pred[92]{0:T(512)(128)(4,1)} %constant.195) | copy-start | bytes 280
  30.7 14.3 %copy-start.2 = (bf16[16,2,64,128]{3,2,1,0:T(8,128)(2,1)}, bf16[16,2,64,128]{3,2,1,0:T(8,128)(2,1)S(1)}, u32[]{:S(2)}) copy-start(bf16[16,2,64,128]{3,2,1,0:T(8,128)(2,1)S(1)} %gather_fusion) | copy-start | bytes 1572868
  30.7 26.4 %collective-permute-start.1 = (bf16[4,4,2,64,128]{4,3,2,1,0:T(8,128)(2,1)S(1)}, bf16[4,4,2,64,128]{4,3,2,1,0:T(8,128)(2,1)S(1)}, u32[]{:S(2)}, u32[]{:S(2)}) collective-permute-start(bf16[4,4,2,64,128]{4,3,2,1,0:T(8,128)(2,1)S(1)} %bitcast.41), channel_id=1, source_target_pairs={{0,1},{1,2},{2,3},{3,4},{4,5},{5,6},{6,7},{7,8},{8,9},{9,10},{10,1... | collective-permute-start | bytes 1572872 | tf_op jit(solution)/shard_map/ppermute | solution.py:178
  40.0 12.7 %all-to-all-start.1 = ((bf16[16,128,128]{2,1,0:T(8,128)(2,1)}), bf16[16,128,128]{2,1,0:T(8,128)(2,1)S(1)}, u32[]{:S(2)}, u32[]{:S(2)}) async-start(bf16[16,128,128]{2,1,0:T(8,128)(2,1)} %bitcast.34), calls=%async_computation.1 | async-start | bytes 1048576 | tf_op jit(solution)/shard_map/all_to_all | solution.py:173
  52.7 4.5 %copy-start = (bf16[16,128,128]{2,1,0:T(8,128)(2,1)}, bf16[16,128,128]{2,1,0:T(8,128)(2,1)S(1)}, u32[]{:S(2)}) copy-start(bf16[16,128,128]{2,1,0:T(8,128)(2,1)S(1)} %all-to-all-done.1) | copy-start | bytes 1572868
  52.7 31.2 %all-to-all-start.2 = ((bf16[16,2,128,128]{3,2,1,0:T(8,128)(2,1)}), bf16[16,2,128,128]{3,2,1,0:T(8,128)(2,1)}, u32[]{:S(2)}, u32[]{:S(2)}) async-start(bf16[16,2,128,128]{3,2,1,0:T(8,128)(2,1)} %pad_maximum_fusion), calls=%async_computation.2 | async-start | bytes 2097152 | tf_op jit(solution)/shard_map/all_to_all | solution.py:173
  57.1 3.5 %copy-start.9 = (s32[64]{0:T(128)S(1)}, s32[64]{0:T(128)}, u32[]{:S(2)}) copy-start(s32[64]{0:T(128)} %param.11) | copy-start | bytes 772
  57.1 4.2 %copy-start.17 = (s32[1,92]{1,0:T(1,128)S(1)}, s32[1,92]{1,0:T(1,128)}, u32[]{:S(2)}) copy-start(s32[1,92]{1,0:T(1,128)} %constant.198) | copy-start | bytes 1108
  57.1 4.2 %copy-start.18 = (s32[1,92]{1,0:T(1,128)S(1)}, s32[1,92]{1,0:T(1,128)}, u32[]{:S(2)}) copy-start(s32[1,92]{1,0:T(1,128)} %constant.202) | copy-start | bytes 1108
  57.1 4.2 %copy-start.14 = (s32[1,92]{1,0:T(1,128)S(1)}, s32[1,92]{1,0:T(1,128)}, u32[]{:S(2)}) copy-start(s32[1,92]{1,0:T(1,128)} %constant.199) | copy-start | bytes 1108
  57.1 4.2 %copy-start.15 = (pred[1,92]{1,0:T(4,128)(4,1)S(1)}, pred[1,92]{1,0:T(4,128)(4,1)}, u32[]{:S(2)}) copy-start(pred[1,92]{1,0:T(4,128)(4,1)} %constant.200) | copy-start | bytes 280
  57.1 4.2 %copy-start.16 = (pred[1,92]{1,0:T(4,128)(4,1)S(1)}, pred[1,92]{1,0:T(4,128)(4,1)}, u32[]{:S(2)}) copy-start(pred[1,92]{1,0:T(4,128)(4,1)} %constant.201) | copy-start | bytes 280
  57.1 14.3 %copy-start.1 = (bf16[4,4,2,64,128]{4,3,2,1,0:T(8,128)(2,1)}, bf16[4,4,2,64,128]{4,3,2,1,0:T(8,128)(2,1)S(1)}, u32[]{:S(2)}) copy-start(bf16[4,4,2,64,128]{4,3,2,1,0:T(8,128)(2,1)S(1)} %collective-permute-done.1.refs_1_) | copy-start | bytes 1572868
  57.2 14.1 %collective-permute-start.2 = (bf16[4,4,2,64,128]{4,3,2,1,0:T(8,128)(2,1)S(1)}, bf16[4,4,2,64,128]{4,3,2,1,0:T(8,128)(2,1)S(1)}, u32[]{:S(2)}, u32[]{:S(2)}) collective-permute-start(bf16[4,4,2,64,128]{4,3,2,1,0:T(8,128)(2,1)S(1)} %pad_maximum_fusion.2), channel_id=1, source_target_pairs={{0,2},{1,3},{2,4},{3,5},{4,6},{5,7},{6,8},{7,9},{8,10},{9,11},{10,... | collective-permute-start | bytes 1572872 | tf_op jit(solution)/shard_map/ppermute | solution.py:178
  71.3 4.7 %copy-start.3 = (bf16[4,4,2,64,128]{4,3,2,1,0:T(8,128)(2,1)}, bf16[4,4,2,64,128]{4,3,2,1,0:T(8,128)(2,1)S(1)}, u32[]{:S(2)}) copy-start(bf16[4,4,2,64,128]{4,3,2,1,0:T(8,128)(2,1)S(1)} %collective-permute-done.2.refs_0_) | copy-start | bytes 1572868
  71.4 14.4 %copy-start.11 = (pred[92]{0:T(512)(128)(4,1)S(1)}, pred[92]{0:T(512)(128)(4,1)}, u32[]{:S(2)}) copy-start(pred[92]{0:T(512)(128)(4,1)} %constant.205) | copy-start | bytes 280
  71.4 14.4 %copy-start.12 = (pred[92]{0:T(512)(128)(4,1)S(1)}, pred[92]{0:T(512)(128)(4,1)}, u32[]{:S(2)}) copy-start(pred[92]{0:T(512)(128)(4,1)} %constant.207) | copy-start | bytes 280
  71.4 14.4 %copy-start.13 = (s32[92]{0:T(128)S(1)}, s32[92]{0:T(128)}, u32[]{:S(2)}) copy-start(s32[92]{0:T(128)} %constant.208) | copy-start | bytes 1108
  71.5 14.7 %copy-start.7 = (s32[64,16,16]{0,2,1:T(8,128)S(1)}, s32[64,16,16]{0,2,1:T(8,128)}, u32[]{:S(2)}) copy-start(s32[64,16,16]{0,2,1:T(8,128)} %param.10) | copy-start | bytes 196612
  71.5 44.6 %collective-permute-start.8 = (bf16[4,8,2,64,128]{4,3,2,1,0:T(8,128)(2,1)S(1)}, bf16[4,8,2,64,128]{4,3,2,1,0:T(8,128)(2,1)}, u32[]{:S(2)}, u32[]{:S(2)}) collective-permute-start(bf16[4,8,2,64,128]{4,3,2,1,0:T(8,128)(2,1)S(1)} %pad_maximum_fusion.1), channel_id=1, source_target_pairs={{0,64},{64,0},{1,65},{65,1},{2,66},{66,2},{3,67},{67,3},{4,68},{68... | collective-permute-start | bytes 3145736 | tf_op jit(solution)/shard_map/ppermute | solution.py:310
  76.1 16.8 %collective-permute-start.3 = (bf16[4,3,2,64,128]{4,3,2,1,0:T(8,128)(2,1)S(1)}, bf16[4,3,2,64,128]{4,3,2,1,0:T(8,128)(2,1)S(1)}, u32[]{:S(2)}, u32[]{:S(2)}) collective-permute-start(bf16[4,3,2,64,128]{4,3,2,1,0:T(8,128)(2,1)S(1)} %pad_maximum_fusion.3), channel_id=1, source_target_pairs={{0,3},{1,4},{2,5},{3,6},{4,7},{5,8},{6,9},{7,10},{8,11},{9,12},{10... | collective-permute-start | bytes 1179656 | tf_op jit(solution)/shard_map/ppermute | solution.py:178
  83.9 43.9 %collective-permute-start.6 = (bf16[4,4,2,128,128]{4,3,2,1,0:T(8,128)(2,1)}, bf16[4,4,2,128,128]{4,3,2,1,0:T(8,128)(2,1)}, u32[]{:S(2)}, u32[]{:S(2)}) collective-permute-start(bf16[4,4,2,128,128]{4,3,2,1,0:T(8,128)(2,1)} %bitcast.18.refs_0_), channel_id=1, source_target_pairs={{0,64},{64,0},{1,65},{65,1},{2,66},{66,2},{3,67},{67,3},{4,68},{68... | collective-permute-start | bytes 3145736 | tf_op jit(solution)/shard_map/ppermute | solution.py:202
  92.9 20.7 %copy-start.6 = (bf16[4,3,2,64,128]{4,3,2,1,0:T(8,128)(2,1)}, bf16[4,3,2,64,128]{4,3,2,1,0:T(8,128)(2,1)S(1)}, u32[]{:S(2)}) copy-start(bf16[4,3,2,64,128]{4,3,2,1,0:T(8,128)(2,1)S(1)} %collective-permute-done.3.refs_2_) | copy-start | bytes 1179652
  92.9 20.7 %collective-permute-start.4 = (bf16[4,2,2,64,128]{4,3,2,1,0:T(8,128)(2,1)S(1)}, bf16[4,2,2,64,128]{4,3,2,1,0:T(8,128)(2,1)S(1)}, u32[]{:S(2)}, u32[]{:S(2)}) collective-permute-start(bf16[4,2,2,64,128]{4,3,2,1,0:T(8,128)(2,1)S(1)} %slice.67), channel_id=1, source_target_pairs={{0,3},{1,4},{2,5},{3,6},{4,7},{5,8},{6,9},{7,10},{8,11},{9,12},{10... | collective-permute-start | bytes 786440 | tf_op jit(solution)/shard_map/ppermute | solution.py:178
  102.8 24.9 %collective-permute-start.7 = (bf16[4,3,2,64,128]{4,3,2,1,0:T(8,128)(2,1)S(1)}, bf16[4,3,2,64,128]{4,3,2,1,0:T(8,128)(2,1)S(1)}, u32[]{:S(2)}, u32[]{:S(2)}) collective-permute-start(bf16[4,3,2,64,128]{4,3,2,1,0:T(8,128)(2,1)S(1)} %collective-permute-done.3.refs_2_), channel_id=1, source_target_pairs={{0,64},{64,0},{1,65},{65,1},{2,66},{66,2},{3,67},{67,3},{4,68},{68... | collective-permute-start | bytes 1179656 | tf_op jit(solution)/shard_map/ppermute | solution.py:311
  113.6 14.1 %copy-start.4 = (bf16[4,2,2,64,128]{4,3,2,1,0:T(8,128)(2,1)}, bf16[4,2,2,64,128]{4,3,2,1,0:T(8,128)(2,1)S(1)}, u32[]{:S(2)}) copy-start(bf16[4,2,2,64,128]{4,3,2,1,0:T(8,128)(2,1)S(1)} %collective-permute-done.4.refs_0_) | copy-start | bytes 786436
  113.6 28.6 %collective-permute-start.5 = (bf16[4,1,2,64,128]{4,3,2,1,0:T(8,128)(2,1)S(1)}, bf16[4,1,2,64,128]{4,3,2,1,0:T(8,128)(2,1)S(1)}, u32[]{:S(2)}, u32[]{:S(2)}) collective-permute-start(bf16[4,1,2,64,128]{4,3,2,1,0:T(8,128)(2,1)S(1)} %slice.68), channel_id=1, source_target_pairs={{0,64},{64,0},{1,65},{65,1},{2,66},{66,2},{3,67},{67,3},{4,68},{68... | collective-permute-start | bytes 393224 | tf_op jit(solution)/shard_map/ppermute | solution.py:312
  (2 other events, 1.4 us)
